TPU v7x, 32 devices: a whole 2x2x4 slice. The times are simulated.
32 devices in a mesh: dp: 4 (over y, x), seq: 4 (over z), feat: 2 (over core).
Axes of the slice: x: 2, y: 2, z: 4, core: 2. Of those that a mesh axis runs over, the one named last changes fastest.
Arguments:
- tokens: bfloat16 [16384, 2048], P(('dp', 'seq')), parts along dimension 0, may hold values from -6 to 6
- w_query: bfloat16 [2048, 256], P(None, 'feat'), may hold values from -0.125 to 0.125
- w_key: bfloat16 [2048, 256], P(None, 'feat'), may hold values from -0.125 to 0.125
- value_weight: bfloat16 [2048, 2048], P(None, 'feat'), may hold values from -0.125 to 0.125
- w_out: bfloat16 [2048, 2048], P(None, 'feat'), may hold values from -0.125 to 0.125
Outputs:
- mixed: bfloat16 [16384, 2048], P(('dp', 'seq'), 'feat'), parts along dimension 0
There are 4 independent parts, one for each index of `dp`. A program takes and returns all parts, laid end to end along the dimension named above; an argument that names none is the same for every part. Nothing has to cross between parts.
All inputs are finite; a program needn't handle non-finite values.
Results may differ from a plain program's by a relative error of at most 0.009.
Values may be sent and summed in bfloat16 or wider, within the bound.
No kernel may reach another device: no remote copies, remote signals or barrier semaphores. Data moves between devices by JAX's collectives and lax.ppermute only.
A program may use at most 64 MiB of HBM per device.

v0:
```python
import jax
import jax.numpy as jnp
from jax import lax
from jax.sharding import PartitionSpec as P

DK = 16
DV = 128


def key_features(key_rows):
    as_float = key_rows.astype(jnp.float32)
    row_count = key_rows.shape[0]
    head_total = key_rows.shape[1]
    linear = jnp.transpose(as_float, (1, 2, 0))
    square = jnp.einsum("nha,nhb->habn", as_float, as_float).reshape(head_total, -1, row_count)
    ones_row = jnp.ones((head_total, 1, row_count), jnp.float32)
    return jnp.concatenate([ones_row, linear, square], axis=1).astype(jnp.bfloat16)


def query_features(query_rows):
    as_float = query_rows.astype(jnp.float32)
    row_count = query_rows.shape[0]
    head_total = query_rows.shape[1]
    linear = jnp.transpose(as_float, (1, 2, 0)) * 0.25
    square = jnp.einsum("nha,nhb->habn", as_float, as_float).reshape(head_total, -1, row_count) * (
        1.0 / 32.0
    )
    ones_row = jnp.ones((head_total, 1, row_count), jnp.float32)
    return jnp.concatenate([ones_row, linear, square], axis=1)


def local(tokens, w_query, w_key, value_weight, w_out):
    row_count = tokens.shape[0]
    local_heads = value_weight.shape[1] // DV
    query_rows = (
        jnp.dot(tokens, w_query, preferred_element_type=jnp.float32)
        .astype(jnp.bfloat16)
        .reshape(row_count, local_heads, DK)
    )
    key_rows = (
        jnp.dot(tokens, w_key, preferred_element_type=jnp.float32)
        .astype(jnp.bfloat16)
        .reshape(row_count, local_heads, DK)
    )
    value_matrix = (
        jnp.dot(tokens, value_weight, preferred_element_type=jnp.float32)
        .astype(jnp.bfloat16)
        .reshape(row_count, local_heads, DV)
    )
    block_state = jnp.einsum(
        "hfn,nhd->hfd", key_features(key_rows), value_matrix, preferred_element_type=jnp.float32
    )
    zero_state = jnp.zeros(block_state.shape, jnp.float32)
    my_block = lax.axis_index("seq")
    piece = lax.all_gather(
        block_state[None].astype(jnp.bfloat16), "seq", axis=0, tiled=True
    ).astype(jnp.float32)
    order = lax.broadcasted_iota(jnp.int32, (piece.shape[0],), 0)
    keep = (order < my_block).astype(jnp.float32)
    earlier = zero_state + jnp.sum(piece * keep[:, None, None, None], axis=0)
    scores = (
        jnp.einsum("nha,mha->hnm", query_rows, key_rows, preferred_element_type=jnp.float32) * 0.25
    )
    causal = lax.broadcasted_iota(jnp.int32, (row_count, row_count), 0) >= lax.broadcasted_iota(
        jnp.int32, (row_count, row_count), 1
    )
    weight_tensors = jnp.where(causal[None], 1.0 + scores + 0.5 * scores * scores, 0.0).astype(
        jnp.bfloat16
    )
    local_portion = jnp.einsum(
        "iot,tiw->oiw", weight_tensors, value_matrix, preferred_element_type=jnp.float32
    )
    carried = jnp.einsum(
        "hfn,hfd->nhd", query_features(query_rows), earlier, precision=lax.Precision.HIGHEST
    )
    numerator = carried + local_portion
    scale = lax.rsqrt(jnp.mean(numerator * numerator, axis=-1, keepdims=True) + 1e-06)
    normalized_rows = (numerator * scale).reshape(row_count, local_heads * DV).astype(jnp.bfloat16)
    mixed = jnp.dot(
        lax.all_gather(normalized_rows, "feat", axis=1, tiled=True),
        w_out,
        preferred_element_type=jnp.float32,
    )
    return mixed.astype(jnp.bfloat16)


def solution(mesh):
    placed = (
        P(("dp", "seq"), None),
        P(None, "feat"),
        P(None, "feat"),
        P(None, "feat"),
        P(None, "feat"),
    )
    return jax.shard_map(
        local, mesh=mesh, in_specs=placed, out_specs=P(("dp", "seq"), "feat"), check_vma=False
    )
```

profile of v0, /device:TPU:0, one launch (start us, length us, event | category | flops | bytes accessed | tf_op | source)
XLA Modules:
  0.0 135.8 jit_solution(15695235256979759861)
XLA Ops:
  6.5 0.0 copy-start
  6.5 1.0 copy-done
  7.6 3.9 %convolution_convert_fusion.3 = bf16[1024,128]{0,1:T(8,128)(2,1)S(1)} fusion(bf16[1024,2048]{1,0:T(8,128)(2,1)} %param.5, bf16[2048,128]{1,0:T(8,128)(2,1)S(1)} %copy-done), kind=kOutput, calls=%fused_computation.30 | convolution fusion | flops 537001984 | bytes 4980736 | tf_op jit(solution)/shard_map/dot_general | solution.py:41
  11.4 0.0 copy-start.1
  11.5 1.3 multiply_convert_fusion
  12.8 0.8 copy-done.1
  13.6 4.8 %convolution_convert_fusion.1 = bf16[1024,1024]{0,1:T(8,128)(2,1)S(1)} fusion(bf16[1024,2048]{1,0:T(8,128)(2,1)S(1)} %copy-done.1, bf16[2048,1024]{1,0:T(8,128)(2,1)S(1)} %copy-done.3), kind=kOutput, calls=%fused_computation.27 | convolution fusion | flops 4296015872 | bytes 10485760 | tf_op jit(solution)/shard_map/dot_general | solution.py:46
  18.5 0.0 copy-start.4
  18.5 0.0 copy-start.2
  18.5 1.7 %fusion.20 = bf16[8,273,128]{2,1,0:T(8,128)(2,1)S(1)} fusion(bf16[1024,8,128]{0,2,1:T(8,128)(2,1)S(1)} %bitcast.51, bf16[8,256,1024]{2,1,0:T(8,128)(2,1)S(1)} %bitcast.47, bf16[8,16,1024]{2,1,0:T(8,128)(2,1)S(1)} %bitcast.49, bf16[273]{0:T(512)(128)(2,1)S(1)} %pad.3.clone), kind=kOutput, calls=%fused_computation.28 | convolution fusion | flops 586220544 | bytes 7113250 | tf_op jit(solution)/shard_map/hfn,nhd->hfd/dot_general | solution.py:50
  20.2 0.9 copy.10
  21.1 0.0 all-gather.6.cloned.1.call-update
  21.1 0.0 all-gather.4.cloned.1.call-start
  21.2 0.3 iota_compare_fusion
  21.5 3.7 %convolution_convert_fusion.2 = bf16[1024,128]{0,1:T(8,128)(2,1)S(1)} fusion(bf16[1024,2048]{1,0:T(8,128)(2,1)} %param.5, bf16[2048,128]{1,0:T(8,128)(2,1)S(1)} %copy-done.2), kind=kOutput, calls=%fused_computation.29 | convolution fusion | flops 537001984 | bytes 4980736 | tf_op jit(solution)/shard_map/dot_general | solution.py:36
  25.3 4.4 %multiply_multiply_fusion = f32[8,1024,16,16]{1,2,3,0:T(8,128)} fusion(f32[8,1024,16]{1,2,0:T(8,128)S(1)} %convert_bitcast_fusion), kind=kLoop, calls=%fused_computation.8 | loop fusion | flops 4194304 | bytes 8912896 | tf_op jit(solution)/shard_map/mul | solution.py:25
  29.8 42.7 %all-gather.6.cloned.1.call-done = bf16[32,273,128]{2,0,1:T(8,128)(2,1)} async-done(((bf16[8,273,128]{2,0,1:T(8,128)(2,1)}), bf16[32,273,128]{2,0,1:T(8,128)(2,1)}) %all-gather.6.cloned.1.call-update) | async-done | bytes 2236432 | tf_op jit(solution)/shard_map/all_gather | solution.py:55
  72.5 2.8 %fusion.13 = f32[8,273,128]{2,0,1:T(8,128)S(1)} fusion(bf16[32,273,128]{2,0,1:T(8,128)(2,1)} %all-gather.6.cloned.1.call-done, f32[4]{0:T(128)S(1)} %compare_convert_fusion), kind=kLoop, calls=%fused_computation.17 | loop fusion | flops 3075072 | bytes 3354640 | tf_op jit(solution)/shard_map/reduce_sum | solution.py:60
  75.4 12.1 %fusion.2 = f32[8,128,1024]{2,1,0:T(8,128)} fusion(f32[8,256,1024]{2,1,0:T(8,128)} %bitcast.45, f32[8,16,1024]{2,1,0:T(8,128)S(1)} %fusion.24, f32[273]{0:T(512)S(1)} %pad.clone, f32[8,273,128]{2,0,1:T(8,128)S(1)} %fusion.13), kind=kOutput, calls=%fused_computation.3 | convolution fusion | flops 3439607808 | bytes 14226500 | tf_op jit(solution)/shard_map/hfn,hfd->nhd/dot_general | solution.py:73
  87.4 16.0 %fusion.14 = (f32[1024,8]{0,1:T(8,128)S(1)}, f32[8,128,1024]{2,1,0:T(8,128)}) fusion(f32[8,128,1024]{2,1,0:T(8,128)} %fusion.2, bf16[1024,8,128]{0,2,1:T(8,128)(2,1)} %bitcast.52, pred[1024,1024]{1,0:T(8,128)(4,1)S(1)} %iota_compare_fusion, bf16[1024,8,16]{0,2,1:T(8,128)(2,1)S(1)} %bitcast.48, bf16[1024,8,16]{0,2,1:T(8,128)(2,1)S(1)} %bitcast.50), kind=kOutput, calls=%fused_computation.20 | convolution fusion | flops 2477776896 | bytes 12091392 | tf_op jit(solution)/shard_map/iot,tiw->oiw/dot_general | solution.py:70
  103.4 4.1 %fusion.15 = bf16[1024,8,128]{0,2,1:T(8,128)(2,1)} fusion(f32[8,128,1024]{2,1,0:T(8,128)} %get-tuple-element.6, f32[1024,8]{0,1:T(8,128)S(1)} %add_rsqrt_fusion), kind=kLoop, calls=%fused_computation.21 | loop fusion | flops 2097152 | bytes 6324224 | tf_op jit(solution)/shard_map/convert_element_type | solution.py:78
  107.5 0.0 all-gather.4.cloned.1.call-update
  107.6 12.0 %all-gather.4.cloned.1.call-done = bf16[1024,2048]{0,1:T(8,128)(2,1)} async-done(((bf16[1024,1024]{0,1:T(8,128)(2,1)}), bf16[1024,2048]{0,1:T(8,128)(2,1)}) %all-gather.4.cloned.1.call-update) | async-done | bytes 4194320 | tf_op jit(solution)/shard_map/all_gather | solution.py:80
  119.6 9.4 %convolution_convert_fusion = bf16[1024,1024]{1,0:T(8,128)(2,1)} fusion(bf16[1024,2048]{0,1:T(8,128)(2,1)} %all-gather.4.cloned.1.call-done, bf16[2048,1024]{1,0:T(8,128)(2,1)} %param.9), kind=kOutput, calls=%fused_computation.26 | convolution fusion | flops 4296015872 | bytes 10485760 | tf_op jit(solution)/shard_map/dot_general | solution.py:79
  (12 shorter events, 0.2 us)
Async XLA Ops:
  6.5 1.0 copy-start
  6.5 66.0 %all-gather.6.cloned.1.call-start = ((), (), s32[]{:S(2)}) async-start(), calls=%async_computation.1 | async-start | bytes 2795520 | tf_op jit(solution)/shard_map/all_gather | solution.py:55
  7.6 5.2 %copy-start.3 = (bf16[2048,1024]{1,0:T(8,128)(2,1)S(1)}, bf16[2048,1024]{1,0:T(8,128)(2,1)}, u32[]{:S(2)}) copy-start(bf16[2048,1024]{1,0:T(8,128)(2,1)} %param.8) | copy-start | bytes 12582916
  11.4 2.2 %copy-start.1 = (bf16[1024,2048]{1,0:T(8,128)(2,1)S(1)}, bf16[1024,2048]{1,0:T(8,128)(2,1)}, u32[]{:S(2)}) copy-start(bf16[1024,2048]{1,0:T(8,128)(2,1)} %param.5) | copy-start | bytes 12582916
  18.5 1.7 %copy-start.4 = (bf16[1024,1024]{0,1:T(8,128)(2,1)}, bf16[1024,1024]{0,1:T(8,128)(2,1)S(1)}, u32[]{:S(2)}) copy-start(bf16[1024,1024]{0,1:T(8,128)(2,1)S(1)} %convolution_convert_fusion.1) | copy-start | bytes 6291460
  18.5 3.0 %copy-start.2 = (bf16[2048,128]{1,0:T(8,128)(2,1)S(1)}, bf16[2048,128]{1,0:T(8,128)(2,1)}, u32[]{:S(2)}) copy-start(bf16[2048,128]{1,0:T(8,128)(2,1)} %param.6) | copy-start | bytes 1572868
  21.1 98.4 %all-gather.4.cloned.1.call-start = ((), (), s32[]{:S(2)}) async-start(), calls=%async_computation | async-start | bytes 6291456 | tf_op jit(solution)/shard_map/all_gather | solution.py:80
Sparse Core Ops, SparseCore 0:
  21.2 51.2 all-gather.5
  107.7 11.8 all-gather.3
where the time goes:
time: 136 us
  waiting for transfers between devices  54.8 us (40%)
  matrix products  51.5 us (38%)
  between operations  13.5 us (10%)
  other arithmetic  13.1 us (10%)
  local copies, waits for them, and re-layouts  2.79 us (2%)
    all_gather x1, waiting for transfers between devices, local(): lax.all_gather(block_state[None].astype(jnp.bfloat16), 'seq', axis=0, til...  42.7 us
    dot_general x1, matrix products, local(): jnp.einsum('iot,tiw->oiw', weight_tensors, value_matrix, preferred_elemen...  16 us
    dot_general x1, matrix products, local(): jnp.einsum('hfn,hfd->nhd', query_features(query_rows), earlier, precision...  12.1 us
    all_gather x1, waiting for transfers between devices, local(): lax.all_gather(normalized_rows, 'feat', axis=1, tiled=True)  12 us
    dot_general x1, matrix products, local(): jnp.dot(lax.all_gather(normalized_rows, 'feat', axis=1, tiled=True), w_ou...  9.36 us
    dot_general x1, matrix products, local(): jnp.dot(tokens, value_weight, preferred_element_type=jnp.float32)  4.81 us
    mul x1, other arithmetic, query_features(): jnp.einsum('nha,nhb->habn', as_float, as_float)  4.45 us
    convert_element_type x1, other arithmetic, local(): (numerator * scale).reshape(row_count, local_heads * DV)  4.11 us
  transfers between devices with their start and end apart: 2, of which 2 were waited for; matrix products, arithmetic and copies ran while one was open for 6% of the time, Pallas kernels for 0%

commit v1 on v0

v1 whole, which is shorter than its diff:
```python
import functools

import jax
import jax.numpy as jnp
from jax import lax
from jax.experimental import pallas as pl
from jax.experimental.pallas import tpu as pltpu
from jax.sharding import PartitionSpec as P

DK = 16
DV = 128
F32 = jnp.float32
BF16 = jnp.bfloat16


def feature_tiles(rows, linear, square, cross):
    half = DK // 2
    tiles = [rows * linear if linear != 1.0 else rows]
    for shift in range(half):
        other = rows if shift == 0 else pltpu.roll(rows, shift, 0)
        weight = square if shift == 0 else cross
        product = rows * other
        tiles.append(product * weight if weight != 1.0 else product)
    far = rows[:half] * rows[half:]
    one = (lax.broadcasted_iota(jnp.int32, far.shape, 0) == 0).astype(F32)
    tiles.append(jnp.concatenate([far * cross if cross != 1.0 else far, one], axis=0))
    return jnp.concatenate([tile.astype(BF16) for tile in tiles], axis=0)


def feature_count():
    return DK + (DK // 2) * DK + DK


def project_kernel(heads, x_ref, wq_ref, wk_ref, wv_ref, q_ref, kt_ref, v_ref, before_ref, total_ref, state):
    step = pl.program_id(0)

    @pl.when(step == 0)
    def _():
        state[...] = jnp.zeros_like(state)

    x = x_ref[...]
    width = heads * DK
    qk = jnp.dot(x, jnp.concatenate([wq_ref[...], wk_ref[...]], axis=1), preferred_element_type=F32)
    q_ref[...] = qk[:, :width].astype(BF16)
    kt = qk[:, width:].astype(BF16).astype(F32).T
    kt_ref[...] = kt.astype(BF16)
    before_ref[0] = state[...]
    for head in range(heads):
        cols = slice(head * DV, (head + 1) * DV)
        if head % 2 == 0:
            pair = slice(head * DV, (head + 2) * DV)
            v_ref[:, pair] = jnp.dot(x, wv_ref[:, pair], preferred_element_type=F32).astype(BF16)
        phi = feature_tiles(kt[head * DK : (head + 1) * DK], 1.0, 1.0, 1.0)
        state[head] += jnp.dot(phi, v_ref[:, cols], preferred_element_type=F32)
    total_ref[...] = state[...].astype(BF16)


def local_kernel(heads, q_ref, kt_ref, v_ref, num_ref, phi_ref):
    chunk = q_ref.shape[0]
    q = q_ref[...]
    kt = kt_ref[...]
    qf = q.astype(F32)
    qt = qf.T
    quarter = (qf * 0.25).astype(BF16)
    causal = lax.broadcasted_iota(jnp.int32, (chunk, chunk), 0) >= lax.broadcasted_iota(
        jnp.int32, (chunk, chunk), 1
    )
    owner = lax.broadcasted_iota(jnp.int32, kt.shape, 0) // DK
    for head in range(heads):
        keys = jnp.where(owner == head, kt, jnp.zeros_like(kt))
        s = jnp.dot(quarter, keys, preferred_element_type=F32)
        w = jnp.where(causal, 1.0 + s * (1.0 + 0.5 * s), 0.0).astype(BF16)
        cols = slice(head * DV, (head + 1) * DV)
        num_ref[:, cols] = jnp.dot(w, v_ref[:, cols], preferred_element_type=F32)
        phi = feature_tiles(qt[head * DK : (head + 1) * DK], 0.25, 1.0 / 32.0, 1.0 / 16.0)
        phi_ref[head] = phi.T


def carry_kernel(heads, num_ref, phi_ref, before_ref, prefix_ref, out_ref):
    for head in range(heads):
        cols = slice(head * DV, (head + 1) * DV)
        state = (before_ref[0, head] + prefix_ref[head].astype(F32)).astype(BF16)
        num = num_ref[:, cols] + jnp.dot(phi_ref[head], state, preferred_element_type=F32)
        scale = lax.rsqrt(jnp.mean(num * num, axis=-1, keepdims=True) + 1e-6)
        out_ref[:, cols] = (num * scale).astype(BF16)


def mix_kernel(order_ref, own_ref, other_ref, wown_ref, wother_ref, out_ref):
    total = jnp.dot(own_ref[...], wown_ref[...], preferred_element_type=F32)
    total += jnp.dot(other_ref[...], wother_ref[...], preferred_element_type=F32)
    out_ref[...] = total.astype(BF16)


def params(mib):
    return pltpu.CompilerParams(vmem_limit_bytes=mib << 20, dimension_semantics=("arbitrary",))


def project(x, w_query, w_key, value_weight, chunk):
    rows, depth = x.shape
    heads = value_weight.shape[1] // DV
    steps = rows // chunk
    count = feature_count()
    width = heads * DK
    return pl.pallas_call(
        functools.partial(project_kernel, heads),
        grid=(steps,),
        in_specs=[
            pl.BlockSpec((chunk, depth), lambda i: (i, 0)),
            pl.BlockSpec((depth, width), lambda i: (0, 0)),
            pl.BlockSpec((depth, width), lambda i: (0, 0)),
            pl.BlockSpec((depth, heads * DV), lambda i: (0, 0)),
        ],
        out_specs=[
            pl.BlockSpec((chunk, width), lambda i: (i, 0)),
            pl.BlockSpec((width, chunk), lambda i: (0, i)),
            pl.BlockSpec((chunk, heads * DV), lambda i: (i, 0)),
            pl.BlockSpec((1, heads, count, DV), lambda i: (i, 0, 0, 0)),
            pl.BlockSpec((heads, count, DV), lambda i: (0, 0, 0)),
        ],
        out_shape=[
            jax.ShapeDtypeStruct((rows, width), BF16),
            jax.ShapeDtypeStruct((width, rows), BF16),
            jax.ShapeDtypeStruct((rows, heads * DV), BF16),
            jax.ShapeDtypeStruct((steps, heads, count, DV), F32),
            jax.ShapeDtypeStruct((heads, count, DV), BF16),
        ],
        scratch_shapes=[pltpu.VMEM((heads, count, DV), F32)],
        compiler_params=params(32),
        cost_estimate=pl.CostEstimate(
            flops=2 * rows * depth * heads * (DV + 2 * DK), bytes_accessed=12 << 20, transcendentals=0
        ),
        name="project",
    )(x, w_query, w_key, value_weight)


def local_part(q, kt, v, chunk):
    rows, width = q.shape
    heads = width // DK
    count = feature_count()
    return pl.pallas_call(
        functools.partial(local_kernel, heads),
        grid=(rows // chunk,),
        in_specs=[
            pl.BlockSpec((chunk, width), lambda i: (i, 0)),
            pl.BlockSpec((width, chunk), lambda i: (0, i)),
            pl.BlockSpec((chunk, heads * DV), lambda i: (i, 0)),
        ],
        out_specs=[
            pl.BlockSpec((chunk, heads * DV), lambda i: (i, 0)),
            pl.BlockSpec((heads, chunk, count), lambda i: (0, i, 0)),
        ],
        out_shape=[
            jax.ShapeDtypeStruct((rows, heads * DV), F32),
            jax.ShapeDtypeStruct((heads, rows, count), BF16),
        ],
        compiler_params=params(16),
        cost_estimate=pl.CostEstimate(
            flops=4 * rows * chunk * heads * DV, bytes_accessed=8 << 20, transcendentals=0
        ),
        name="local",
    )(q, kt, v)


def carry(num, phi, before, prefix, chunk, first, rows):
    heads, _, count = phi.shape
    return pl.pallas_call(
        functools.partial(carry_kernel, heads),
        grid=(rows // chunk,),
        in_specs=[
            pl.BlockSpec((chunk, heads * DV), lambda i: (i + first, 0)),
            pl.BlockSpec((heads, chunk, count), lambda i: (0, i + first, 0)),
            pl.BlockSpec((1, heads, count, DV), lambda i: (i + first, 0, 0, 0)),
            pl.BlockSpec((heads, count, DV), lambda i: (0, 0, 0)),
        ],
        out_specs=pl.BlockSpec((chunk, heads * DV), lambda i: (i, 0)),
        out_shape=jax.ShapeDtypeStruct((rows, heads * DV), BF16),
        compiler_params=params(16),
        cost_estimate=pl.CostEstimate(
            flops=2 * rows * count * heads * DV, bytes_accessed=4 << 20, transcendentals=0
        ),
        name="carry",
    )(num, phi, before, prefix)


def mix_pair(order, own, other, w_out, tile):
    rows, depth = own.shape
    width = w_out.shape[1]
    grid_spec = pltpu.PrefetchScalarGridSpec(
        num_scalar_prefetch=1,
        grid=(rows // tile,),
        in_specs=[
            pl.BlockSpec((tile, depth), lambda i, o: (i, 0)),
            pl.BlockSpec((tile, depth), lambda i, o: (i, 0)),
            pl.BlockSpec((depth, width), lambda i, o: (o[0], 0)),
            pl.BlockSpec((depth, width), lambda i, o: (o[1], 0)),
        ],
        out_specs=pl.BlockSpec((tile, width), lambda i, o: (i, 0)),
    )
    return pl.pallas_call(
        mix_kernel,
        grid_spec=grid_spec,
        out_shape=jax.ShapeDtypeStruct((rows, width), BF16),
        compiler_params=params(16),
        cost_estimate=pl.CostEstimate(
            flops=4 * rows * depth * width, bytes_accessed=6 << 20, transcendentals=0
        ),
        name="mix",
    )(order, own, other, w_out, w_out)


def swap(value, axis, size, bit):
    return lax.ppermute(value, axis, [(i, i ^ bit) for i in range(size)])


def prefix_of(total, size):
    index = lax.axis_index("seq")
    if size == 1:
        return jnp.zeros_like(total)
    if size == 4:
        odd = (index % 2) == 1
        upper = index >= 2
        half = total.shape[0] // 2
        low, high = total[:half], total[half:]
        zero = jnp.zeros_like(low)
        got = swap(jnp.where(odd, low, high), "seq", size, 1)
        pair = (jnp.where(odd, high, low).astype(F32) + got.astype(F32)).astype(BF16)
        across = jnp.where(upper, swap(pair, "seq", size, 2), zero)
        send = (across.astype(F32) + jnp.where(odd, zero, low).astype(F32)).astype(BF16)
        last = swap(send, "seq", size, 1)
        first = jnp.where(odd, last, across)
        second = jnp.where(odd, got.astype(F32) + across.astype(F32), last.astype(F32)).astype(BF16)
        return jnp.concatenate([first, second], axis=0)
    prefix = jnp.zeros(total.shape, F32)
    if size & (size - 1) == 0:
        running = total.astype(F32)
        bit = 1
        while bit < size:
            got = swap(running.astype(BF16), "seq", size, bit).astype(F32)
            prefix = prefix + jnp.where((index & bit) != 0, got, jnp.zeros_like(got))
            running = running + got
            bit *= 2
        return prefix.astype(BF16)
    moved = total
    for hop in range(1, size):
        moved = lax.ppermute(moved, "seq", [(i, (i + 1) % size) for i in range(size)])
        prefix = prefix + jnp.where(index >= hop, moved.astype(F32), 0.0)
    return prefix.astype(BF16)


def local(seq_size, feat_size, tokens, w_query, w_key, value_weight, w_out):
    rows = tokens.shape[0]
    chunk = min(rows, 256)
    q, kt, v, before, total = project(tokens, w_query, w_key, value_weight, chunk)
    prefix = prefix_of(total, seq_size)
    num, phi = local_part(q, kt, v, chunk)
    if feat_size == 2:
        mine = lax.axis_index("feat").astype(jnp.int32)
        order = jnp.stack([mine, 1 - mine])
        parts = 2 if rows % (2 * chunk) == 0 else 1
        piece = rows // parts
        outs = []
        for part in range(parts):
            normed = carry(num, phi, before, prefix, chunk, part * piece // chunk, piece)
            other = swap(normed, "feat", 2, 1)
            outs.append(mix_pair(order, normed, other, w_out, chunk))
        return jnp.concatenate(outs, axis=0) if parts > 1 else outs[0]
    normed = carry(num, phi, before, prefix, chunk, 0, rows)
    full = lax.all_gather(normed, "feat", axis=1, tiled=True) if feat_size > 1 else normed
    return jnp.dot(full, w_out, preferred_element_type=F32).astype(BF16)


def solution(mesh):
    placed = (
        P(("dp", "seq"), None),
        P(None, "feat"),
        P(None, "feat"),
        P(None, "feat"),
        P(None, "feat"),
    )
    body = functools.partial(local, mesh.shape["seq"], mesh.shape["feat"])
    return jax.shard_map(
        body, mesh=mesh, in_specs=placed, out_specs=P(("dp", "seq"), "feat"), check_vma=False
    )
```

time: 136 us -> 66.6 us (0.49)
  the two profiles are of different devices: /device:TPU:0 before, /device:TPU:19 now
where the time goes in v1:
time: 66.6 us; the launch traced here: 66.3 us
  Pallas kernels  30.1 us (45%)
  local copies, waits for them, and re-layouts  12.2 us (18%)
  waiting for transfers between devices  11.1 us (17%)
  starting transfers between devices  7.49 us (11%)
  other arithmetic  5.29 us (8%)
    pallas_call x1, Pallas kernels, project(): pl.pallas_call(functools.partial(project_kernel, heads), grid=(steps,), i...  13.5 us
    unnamed x20, local copies, waits for them, and re-layouts  12.2 us
    ppermute x5, waiting for transfers between devices, swap(): return lax.ppermute(value, axis, [(i, i ^ bit) for i in range(size)])  11.1 us
    pallas_call x2, Pallas kernels, mix_pair(): pl.pallas_call(mix_kernel, grid_spec=grid_spec, out_shape=jax.ShapeDtypeS...  8.81 us
    ppermute x5, starting transfers between devices, swap(): return lax.ppermute(value, axis, [(i, i ^ bit) for i in range(size)])  7.49 us
    pallas_call x2, Pallas kernels, carry(): pl.pallas_call(functools.partial(carry_kernel, heads), grid=(rows // chun...  4.04 us
    pallas_call x1, Pallas kernels, local_part(): pl.pallas_call(functools.partial(local_kernel, heads), grid=(rows // chun...  3.7 us
    concatenate x1, other arithmetic, local(): return jnp.concatenate(outs, axis=0) if parts > 1 else outs[0]  1.49 us
  transfers between devices with their start and end apart: 5, of which 3 were waited for; matrix products, arithmetic and copies ran while one was open for 0% of the time, Pallas kernels for 16%

profile of v1, /device:TPU:19, one launch (start us, length us, event | category | flops | bytes accessed | tf_op | source)
XLA Modules:
  0.0 66.3 jit_solution(4718515841609219311)
XLA Ops:
  0.0 2.2 %copy-done.2 = bf16[1024,2048]{1,0:T(8,128)(2,1)S(1)} copy-done((bf16[1024,2048]{1,0:T(8,128)(2,1)S(1)}, bf16[1024,2048]{1,0:T(8,128)(2,1)}, u32[]{:S(2)}) %copy-start.2) | copy-done | bytes 4194328
  2.2 2.2 %copy-done.3 = bf16[2048,1024]{1,0:T(8,128)(2,1)S(1)} copy-done((bf16[2048,1024]{1,0:T(8,128)(2,1)S(1)}, bf16[2048,1024]{1,0:T(8,128)(2,1)}, u32[]{:S(2)}) %copy-start.3) | copy-done | bytes 4194328
  4.4 1.0 %copy-done.4 = bf16[2048,128]{1,0:T(8,128)(2,1)S(1)} copy-done((bf16[2048,128]{1,0:T(8,128)(2,1)S(1)}, bf16[2048,128]{1,0:T(8,128)(2,1)}, u32[]{:S(2)}) %copy-start.4) | copy-done | bytes 524312
  5.4 1.0 %copy-done.5 = bf16[2048,128]{1,0:T(8,128)(2,1)S(1)} copy-done((bf16[2048,128]{1,0:T(8,128)(2,1)S(1)}, bf16[2048,128]{1,0:T(8,128)(2,1)}, u32[]{:S(2)}) %copy-start.5) | copy-done | bytes 524312
  6.5 13.5 %project.1 = (bf16[1024,128]{1,0:T(8,128)(2,1)S(1)}, bf16[128,1024]{1,0:T(8,128)(2,1)S(1)}, bf16[1024,1024]{1,0:T(8,128)(2,1)S(1)}, f32[4,8,160,128]{3,2,1,0:T(8,128)S(1)}, bf16[8,160,128]{2,1,0:T(8,128)(2,1)S(1)}) custom-call(bf16[1024,2048]{1,0:T(8,128)(2,1)S(1)} %copy-done.2, bf16[2048,128]{1,0:T(8,128)(2,1)S(1)} %copy-done.4, ...), custom_call_target="tpu_custom_call" | custom-call | flops 5368709120 | bytes 12582912 | tf_op jit(solution)/shard_map/project/pallas_call | solution.py:104
  20.0 1.3 %copy-done.6 = bf16[1024,1024]{1,0:T(8,128)(2,1)} copy-done((bf16[1024,1024]{1,0:T(8,128)(2,1)}, bf16[1024,1024]{1,0:T(8,128)(2,1)S(1)}, u32[]{:S(2)}) %copy-start.6) | copy-done | bytes 2097176
  21.3 1.4 %collective-permute-start = (bf16[4,160,128]{2,1,0:T(8,128)(2,1)S(1)}, bf16[4,160,128]{2,1,0:T(8,128)(2,1)S(1)}, u32[]{:S(2)}, u32[]{:S(2)}) collective-permute-start(bf16[4,160,128]{2,1,0:T(8,128)(2,1)S(1)} %broadcast_select_fusion.2), channel_id=1, source_target_pairs={{0,2},{2,0},{4,6},{6,4},{1,3},{3,1},{5,7},{7,5},{8,10},{10,8},{12,... | collective-permute-start | bytes 491528 | tf_op jit(solution)/shard_map/ppermute | solution.py:212
  22.7 3.8 %collective-permute-done = bf16[4,160,128]{2,1,0:T(8,128)(2,1)S(1)} collective-permute-done((bf16[4,160,128]{2,1,0:T(8,128)(2,1)S(1)}, bf16[4,160,128]{2,1,0:T(8,128)(2,1)S(1)}, u32[]{:S(2)}, u32[]{:S(2)}) %collective-permute-start) | collective-permute-done | bytes 163872 | tf_op jit(solution)/shard_map/ppermute | solution.py:212
  26.5 0.7 %copy-done.8 = bf16[4,160,128]{2,1,0:T(8,128)(2,1)} copy-done((bf16[4,160,128]{2,1,0:T(8,128)(2,1)}, bf16[4,160,128]{2,1,0:T(8,128)(2,1)S(1)}, u32[]{:S(2)}) %copy-start.8) | copy-done | bytes 163864
  27.2 0.7 %fusion = bf16[4,160,128]{2,1,0:T(8,128)(2,1)} fusion(bf16[4,160,128]{2,1,0:T(8,128)(2,1)S(1)} %collective-permute-done, pred[]{:T(512)S(6)} %eq.5, bf16[8,160,128]{2,1,0:T(8,128)(2,1)S(1)} %get-tuple-element.18), kind=kLoop, calls=%fused_computation.4 | loop fusion | flops 409600 | bytes 655361 | tf_op jit(solution)/shard_map/convert_element_type | solution.py:226
  28.0 6.7 %collective-permute-done.1 = bf16[4,160,128]{2,1,0:T(8,128)(2,1)} collective-permute-done((bf16[4,160,128]{2,1,0:T(8,128)(2,1)}, bf16[4,160,128]{2,1,0:T(8,128)(2,1)}, u32[]{:S(2)}, u32[]{:S(2)}) %collective-permute-start.1) | collective-permute-done | bytes 163872 | tf_op jit(solution)/shard_map/ppermute | solution.py:212
  34.7 1.0 %fusion.1 = bf16[4,160,128]{2,1,0:T(8,128)(2,1)S(1)} fusion(pred[]{:T(512)S(6)} %eq.5, bf16[8,160,128]{2,1,0:T(8,128)(2,1)S(1)} %get-tuple-element.18, bf16[4,160,128]{2,1,0:T(8,128)(2,1)} %collective-permute-done.1, pred[]{:T(512)S(6)} %ge.3), kind=kLoop, calls=%fused_computation.5 | loop fusion | flops 491520 | bytes 491522 | tf_op jit(solution)/shard_map/convert_element_type | solution.py:228
  35.7 5.2 %collective-permute-start.2 = (bf16[4,160,128]{2,1,0:T(8,128)(2,1)S(1)}, bf16[4,160,128]{2,1,0:T(8,128)(2,1)S(1)}, u32[]{:S(2)}, u32[]{:S(2)}) collective-permute-start(bf16[4,160,128]{2,1,0:T(8,128)(2,1)S(1)} %fusion.1), channel_id=1, source_target_pairs={{0,2},{2,0},{4,6},{6,4},{1,3},{3,1},{5,7},{7,5},{8,10},{10,8},{12,... | collective-permute-start | bytes 491528 | tf_op jit(solution)/shard_map/ppermute | solution.py:212
  40.8 1.6 %copy-done.7 = bf16[1024,1024]{1,0:T(8,128)(2,1)S(1)} copy-done((bf16[1024,1024]{1,0:T(8,128)(2,1)S(1)}, bf16[1024,1024]{1,0:T(8,128)(2,1)}, u32[]{:S(2)}) %copy-start.7) | copy-done | bytes 2097176
  42.4 3.7 %local.1 = (f32[1024,1024]{1,0:T(8,128)S(1)}, bf16[8,1024,160]{2,1,0:T(8,128)(2,1)S(1)}) custom-call(bf16[1024,128]{1,0:T(8,128)(2,1)S(1)} %get-tuple-element.12.q_ref, bf16[128,1024]{1,0:T(8,128)(2,1)S(1)} %get-tuple-element.13.kt_ref, bf16[1024,1024]{1,0:T(8,128)(2,1)S(1)} %copy-done.7), custom_call_target="tpu_custom_call" | custom-call | flops 1073741824 | bytes 8388608 | tf_op jit(solution)/shard_map/local/pallas_call | solution.py:140
  46.2 1.0 %fusion.3 = bf16[4,160,128]{2,1,0:T(8,128)(2,1)S(1)} fusion(bf16[4,160,128]{2,1,0:T(8,128)(2,1)S(1)} %copy-done.9, bf16[4,160,128]{2,1,0:T(8,128)(2,1)S(1)} %collective-permute-done.2, pred[]{:T(512)S(6)} %eq.5, bf16[4,160,128]{2,1,0:T(8,128)(2,1)} %collective-permute-done.1, pred[]{:T(512)S(6)} %ge.3), kind=kLoop, calls=%fused_computation.7 | loop fusion | flops 573440 | bytes 655362 | tf_op jit(solution)/shard_map/convert_element_type | solution.py:231
  47.2 0.9 %broadcast_select_fusion.1 = bf16[4,160,128]{2,1,0:T(8,128)(2,1)S(1)} fusion(bf16[4,160,128]{2,1,0:T(8,128)(2,1)S(1)} %collective-permute-done.2, pred[]{:T(512)S(6)} %eq.5, bf16[4,160,128]{2,1,0:T(8,128)(2,1)} %collective-permute-done.1, pred[]{:T(512)S(6)} %ge.3), kind=kLoop, calls=%fused_computation.10 | loop fusion | flops 163840 | bytes 491522 | tf_op jit(solution)/shard_map/jit(_where)/select_n | solution.py:230
  48.2 2.0 %carry.2.own_ref = bf16[512,1024]{1,0:T(8,128)(2,1)} custom-call(f32[1024,1024]{1,0:T(8,128)S(1)} %get-tuple-element.15.num_ref, bf16[8,1024,160]{2,1,0:T(8,128)(2,1)S(1)} %get-tuple-element.16.phi_ref, f32[4,8,160,128]{3,2,1,0:T(8,128)S(1)} %get-tuple-element.17.before_ref, bf16[8,160,128]{2,1,0:T(8,128)(2,1)S(1)} %pad_maximum_fusion.1.prefix_ref), custom_call_target="tpu_custom_call" | custom-call | flops 167772160 | bytes 4194304 | tf_op jit(solution)/shard_map/carry/pallas_call | solution.py:166
  50.2 0.9 %collective-permute-start.3 = (bf16[512,1024]{1,0:T(8,128)(2,1)}, bf16[512,1024]{1,0:T(8,128)(2,1)}, u32[]{:S(2)}, u32[]{:S(2)}) collective-permute-start(bf16[512,1024]{1,0:T(8,128)(2,1)} %carry.2.own_ref), channel_id=1, source_target_pairs={{0,1},{1,0},{2,3},{3,2},{4,5},{5,4},{6,7},{7,6},{8,9},{9,8},{10,11... | collective-permute-start | bytes 3145736 | tf_op jit(solution)/shard_map/ppermute | solution.py:212
  51.1 2.0 %carry.3.own_ref = bf16[512,1024]{1,0:T(8,128)(2,1)} custom-call(f32[1024,1024]{1,0:T(8,128)S(1)} %get-tuple-element.15.num_ref, bf16[8,1024,160]{2,1,0:T(8,128)(2,1)S(1)} %get-tuple-element.16.phi_ref, f32[4,8,160,128]{3,2,1,0:T(8,128)S(1)} %get-tuple-element.17.before_ref, bf16[8,160,128]{2,1,0:T(8,128)(2,1)S(1)} %pad_maximum_fusion.1.prefix_ref), custom_call_target="tpu_custom_call" | custom-call | flops 167772160 | bytes 4194304 | tf_op jit(solution)/shard_map/carry/pallas_call | solution.py:166
  53.7 2.2 %copy-done = bf16[2048,1024]{1,0:T(8,128)(2,1)S(1)} copy-done((bf16[2048,1024]{1,0:T(8,128)(2,1)S(1)}, bf16[2048,1024]{1,0:T(8,128)(2,1)}, u32[]{:S(2)}) %copy-start) | copy-done | bytes 4194328
  55.9 4.6 %mix.2 = bf16[512,1024]{1,0:T(8,128)(2,1)S(1)} custom-call(s32[2]{0:T(128)S(1)} %pad_add_fusion.order_ref, bf16[512,1024]{1,0:T(8,128)(2,1)} %carry.2.own_ref, bf16[512,1024]{1,0:T(8,128)(2,1)} %collective-permute-done.3.other_ref, bf16[2048,1024]{1,0:T(8,128)(2,1)S(1)} %copy-done, bf16[2048,1024]{1,0:T(8,128)(2,1)S(1)} %copy-done), custom_call_target="tpu_custom_call" | custom-call | flops 2147483648 | bytes 6291456 | tf_op jit(solution)/shard_map/mix/pallas_call | solution.py:199
  60.6 4.2 %mix.3 = bf16[512,1024]{1,0:T(8,128)(2,1)S(1)} custom-call(s32[2]{0:T(128)S(1)} %pad_add_fusion.order_ref, bf16[512,1024]{1,0:T(8,128)(2,1)} %carry.3.own_ref, bf16[512,1024]{1,0:T(8,128)(2,1)S(1)} %collective-permute-done.4.other_ref, bf16[2048,1024]{1,0:T(8,128)(2,1)S(1)} %copy-done.1, bf16[2048,1024]{1,0:T(8,128)(2,1)S(1)} %copy-done.1), custom_call_target="tpu_custom_call" | custom-call | flops 2147483648 | bytes 6291456 | tf_op jit(solution)/shard_map/mix/pallas_call | solution.py:199
  64.8 1.5 %pad_maximum_fusion = bf16[1024,1024]{1,0:T(8,128)(2,1)} fusion(bf16[512,1024]{1,0:T(8,128)(2,1)S(1)} %mix.3, bf16[512,1024]{1,0:T(8,128)(2,1)S(1)} %mix.2), kind=kLoop, calls=%fused_computation | loop fusion | flops 4194304 | bytes 4194304 | tf_op jit(solution)/shard_map/concatenate | solution.py:266
  (20 shorter events, 0.7 us)
Async XLA Ops:
  0.0 2.2 %copy-start.2 = (bf16[1024,2048]{1,0:T(8,128)(2,1)S(1)}, bf16[1024,2048]{1,0:T(8,128)(2,1)}, u32[]{:S(2)}) copy-start(bf16[1024,2048]{1,0:T(8,128)(2,1)} %x_ref.1) | copy-start | bytes 12582916
  2.2 2.2 %copy-start.3 = (bf16[2048,1024]{1,0:T(8,128)(2,1)S(1)}, bf16[2048,1024]{1,0:T(8,128)(2,1)}, u32[]{:S(2)}) copy-start(bf16[2048,1024]{1,0:T(8,128)(2,1)} %wv_ref.1) | copy-start | bytes 12582916
  4.4 1.0 %copy-start.4 = (bf16[2048,128]{1,0:T(8,128)(2,1)S(1)}, bf16[2048,128]{1,0:T(8,128)(2,1)}, u32[]{:S(2)}) copy-start(bf16[2048,128]{1,0:T(8,128)(2,1)} %wq_ref.1) | copy-start | bytes 1572868
  5.4 1.0 %copy-start.5 = (bf16[2048,128]{1,0:T(8,128)(2,1)S(1)}, bf16[2048,128]{1,0:T(8,128)(2,1)}, u32[]{:S(2)}) copy-start(bf16[2048,128]{1,0:T(8,128)(2,1)} %wk_ref.1) | copy-start | bytes 1572868
  20.0 1.3 %copy-start.6 = (bf16[1024,1024]{1,0:T(8,128)(2,1)}, bf16[1024,1024]{1,0:T(8,128)(2,1)S(1)}, u32[]{:S(2)}) copy-start(bf16[1024,1024]{1,0:T(8,128)(2,1)S(1)} %get-tuple-element.14.v_ref) | copy-start | bytes 6291460
  21.3 5.1 %collective-permute-start = (bf16[4,160,128]{2,1,0:T(8,128)(2,1)S(1)}, bf16[4,160,128]{2,1,0:T(8,128)(2,1)S(1)}, u32[]{:S(2)}, u32[]{:S(2)}) collective-permute-start(bf16[4,160,128]{2,1,0:T(8,128)(2,1)S(1)} %broadcast_select_fusion.2), channel_id=1, source_target_pairs={{0,2},{2,0},{4,6},{6,4},{1,3},{3,1},{5,7},{7,5},{8,10},{10,8},{12,... | collective-permute-start | bytes 491528 | tf_op jit(solution)/shard_map/ppermute | solution.py:212
  26.5 0.7 %copy-start.8 = (bf16[4,160,128]{2,1,0:T(8,128)(2,1)}, bf16[4,160,128]{2,1,0:T(8,128)(2,1)S(1)}, u32[]{:S(2)}) copy-start(bf16[4,160,128]{2,1,0:T(8,128)(2,1)S(1)} %collective-permute-done) | copy-start | bytes 491524
  27.9 6.8 %collective-permute-start.1 = (bf16[4,160,128]{2,1,0:T(8,128)(2,1)}, bf16[4,160,128]{2,1,0:T(8,128)(2,1)}, u32[]{:S(2)}, u32[]{:S(2)}) collective-permute-start(bf16[4,160,128]{2,1,0:T(8,128)(2,1)} %fusion), channel_id=1, source_target_pairs={{0,4},{2,6},{4,0},{6,2},{1,5},{3,7},{5,1},{7,3},{8,12},{10,14},{12... | collective-permute-start | bytes 491528 | tf_op jit(solution)/shard_map/ppermute | solution.py:212
  28.0 18.2 %copy-start.9 = (bf16[4,160,128]{2,1,0:T(8,128)(2,1)S(1)}, bf16[4,160,128]{2,1,0:T(8,128)(2,1)}, u32[]{:S(2)}) copy-start(bf16[4,160,128]{2,1,0:T(8,128)(2,1)} %copy-done.8) | copy-start | bytes 491524
  35.7 10.5 %collective-permute-start.2 = (bf16[4,160,128]{2,1,0:T(8,128)(2,1)S(1)}, bf16[4,160,128]{2,1,0:T(8,128)(2,1)S(1)}, u32[]{:S(2)}, u32[]{:S(2)}) collective-permute-start(bf16[4,160,128]{2,1,0:T(8,128)(2,1)S(1)} %fusion.1), channel_id=1, source_target_pairs={{0,2},{2,0},{4,6},{6,4},{1,3},{3,1},{5,7},{7,5},{8,10},{10,8},{12,... | collective-permute-start | bytes 491528 | tf_op jit(solution)/shard_map/ppermute | solution.py:212
  40.8 1.6 %copy-start.7 = (bf16[1024,1024]{1,0:T(8,128)(2,1)S(1)}, bf16[1024,1024]{1,0:T(8,128)(2,1)}, u32[]{:S(2)}) copy-start(bf16[1024,1024]{1,0:T(8,128)(2,1)} %copy-done.6) | copy-start | bytes 6291460
  50.2 3.5 %collective-permute-start.3 = (bf16[512,1024]{1,0:T(8,128)(2,1)}, bf16[512,1024]{1,0:T(8,128)(2,1)}, u32[]{:S(2)}, u32[]{:S(2)}) collective-permute-start(bf16[512,1024]{1,0:T(8,128)(2,1)} %carry.2.own_ref), channel_id=1, source_target_pairs={{0,1},{1,0},{2,3},{3,2},{4,5},{5,4},{6,7},{7,6},{8,9},{9,8},{10,11... | collective-permute-start | bytes 3145736 | tf_op jit(solution)/shard_map/ppermute | solution.py:212
  53.1 7.4 %collective-permute-start.4 = (bf16[512,1024]{1,0:T(8,128)(2,1)}, bf16[512,1024]{1,0:T(8,128)(2,1)S(1)}, u32[]{:S(2)}, u32[]{:S(2)}) collective-permute-start(bf16[512,1024]{1,0:T(8,128)(2,1)} %carry.3.own_ref), channel_id=1, source_target_pairs={{0,1},{1,0},{2,3},{3,2},{4,5},{5,4},{6,7},{7,6},{8,9},{9,8},{10,11... | collective-permute-start | bytes 3145736 | tf_op jit(solution)/shard_map/ppermute | solution.py:212
  53.7 2.2 %copy-start = (bf16[2048,1024]{1,0:T(8,128)(2,1)S(1)}, bf16[2048,1024]{1,0:T(8,128)(2,1)}, u32[]{:S(2)}) copy-start(bf16[2048,1024]{1,0:T(8,128)(2,1)} %wother_ref.3) | copy-start | bytes 12582916
  55.9 4.6 %copy-start.1 = (bf16[2048,1024]{1,0:T(8,128)(2,1)S(1)}, bf16[2048,1024]{1,0:T(8,128)(2,1)}, u32[]{:S(2)}) copy-start(bf16[2048,1024]{1,0:T(8,128)(2,1)} %wother_ref.3) | copy-start | bytes 12582916

commit v2 on v1

v2 whole, which is shorter than its diff:
```python
import functools

import jax
import jax.numpy as jnp
from jax import lax
from jax.experimental import pallas as pl
from jax.experimental.pallas import tpu as pltpu
from jax.sharding import PartitionSpec as P

DK = 16
DV = 128
F32 = jnp.float32
BF16 = jnp.bfloat16


def feature_tiles(rows, linear, square, cross):
    half = DK // 2
    tiles = [rows * linear if linear != 1.0 else rows]
    for shift in range(half):
        other = rows if shift == 0 else pltpu.roll(rows, shift, 0)
        weight = square if shift == 0 else cross
        product = rows * other
        tiles.append(product * weight if weight != 1.0 else product)
    far = rows[:half] * rows[half:]
    one = (lax.broadcasted_iota(jnp.int32, far.shape, 0) == 0).astype(F32)
    tiles.append(jnp.concatenate([far * cross if cross != 1.0 else far, one], axis=0))
    return jnp.concatenate([tile.astype(BF16) for tile in tiles], axis=0)


def feature_count():
    return DK + (DK // 2) * DK + DK


VMEM = pl.BlockSpec(memory_space=pltpu.VMEM)
HBM = pl.BlockSpec(memory_space=pltpu.HBM)
SMEM = pl.BlockSpec(memory_space=pltpu.SMEM)


def in_hbm(value):
    return pltpu.with_memory_space_constraint(value, pltpu.HBM)


def span(index, size):
    return slice(index * size, (index + 1) * size)


def halves(count):
    middle = max(count // 2, 1)
    return range(middle), range(middle, count)


def project_kernel(
    heads, chunk, x_in, wq_in, wk_in, wv_in, q_ref, kt_ref, v_ref, before_ref, total_ref, x_ref, wq_ref, wk_ref, wv_ref, sems
):
    steps = x_in.shape[0] // chunk
    width = heads * DK
    group = 2 if heads % 2 == 0 else 1
    groups = heads // group
    cols = group * DV
    copies = {}

    def fetch(key, source, target):
        copies[key] = pltpu.make_async_copy(source, target, sems.at[len(copies)])
        copies[key].start()

    def fetch_x(m):
        rows = pl.ds(m * chunk, chunk)
        fetch(("x", m), x_in.at[rows], x_ref.at[rows])

    def wait(keys):
        for key in keys:
            copies[key].wait()

    def project_qk(m):
        rows = span(m, chunk)
        both = jnp.concatenate([wq_ref[...], wk_ref[...]], axis=1)
        qk = jnp.dot(x_ref[rows, :], both, preferred_element_type=F32)
        q_ref[rows, :] = qk[:, :width].astype(BF16)
        kt_ref[:, rows] = qk[:, width:].T.astype(BF16)

    def add_states(m, g):
        rows = span(m, chunk)
        for head in range(g * group, (g + 1) * group):
            keys = kt_ref[span(head, DK), rows].astype(F32)
            phi = feature_tiles(keys, 1.0, 1.0, 1.0)
            new = jnp.dot(phi, v_ref[rows, span(head, DV)], preferred_element_type=F32)
            if m > 0:
                new = before_ref[m - 1, head] + new
            if m < steps - 1:
                before_ref[m, head] = new
            else:
                total_ref[head] = new.astype(BF16)

    pending = []

    def project_v(m, g):
        rows = span(m, chunk)
        v_ref[rows, span(g, cols)] = jnp.dot(
            x_ref[rows, :], wv_ref[:, span(g, cols)], preferred_element_type=F32
        ).astype(BF16)
        pending.append((m, g))
        if len(pending) > 1:
            add_states(*pending.pop(0))

    early, late = halves(steps)
    fetch("q", wq_in, wq_ref)
    fetch("k", wk_in, wk_ref)
    for m in early:
        fetch_x(m)
    for g in range(groups):
        pair = pl.ds(g * cols, cols)
        fetch(("v", g), wv_in.at[:, pair], wv_ref.at[:, pair])
    for m in late:
        fetch_x(m)
    wait(["q", "k"] + [("x", m) for m in early])
    for m in early:
        project_qk(m)
    for part in halves(groups):
        wait([("v", g) for g in part])
        for m in early:
            for g in part:
                project_v(m, g)
    wait([("x", m) for m in late])
    for m in late:
        project_qk(m)
        for g in range(groups):
            project_v(m, g)
    for item in pending:
        add_states(*item)


def local_kernel(heads, chunk, q_ref, kt_ref, v_ref, w_in, num_ref, phi_ref, w_ref, sem):
    fetch = pltpu.make_async_copy(w_in, w_ref, sem)
    fetch.start()
    causal = lax.broadcasted_iota(jnp.int32, (chunk, chunk), 0) >= lax.broadcasted_iota(
        jnp.int32, (chunk, chunk), 1
    )
    owner = lax.broadcasted_iota(jnp.int32, (kt_ref.shape[0], chunk), 0) // DK
    for m in range(q_ref.shape[0] // chunk):
        rows = span(m, chunk)
        kt = kt_ref[:, rows]
        q = q_ref[rows, :].astype(F32)
        qt = q.T
        quarter = (q * 0.25).astype(BF16)
        for head in range(heads):
            keys = jnp.where(owner == head, kt, jnp.zeros_like(kt))
            s = jnp.dot(quarter, keys, preferred_element_type=F32)
            w = jnp.where(causal, 1.0 + s * (1.0 + 0.5 * s), 0.0).astype(BF16)
            cols = span(head, DV)
            num_ref[rows, cols] = jnp.dot(w, v_ref[rows, cols], preferred_element_type=F32)
            phi = feature_tiles(qt[span(head, DK)], 0.25, 1.0 / 32.0, 1.0 / 16.0)
            phi_ref[head, rows] = phi.T
    fetch.wait()


def carry_kernel(heads, chunk, first, num_ref, phi_ref, before_ref, prefix_ref, out_ref):
    for step in range(out_ref.shape[0] // chunk):
        m = first + step
        rows = span(m, chunk)
        for head in range(heads):
            cols = span(head, DV)
            state = prefix_ref[head]
            if m > 0:
                state = (state.astype(F32) + before_ref[m - 1, head]).astype(BF16)
            num = num_ref[rows, cols] + jnp.dot(phi_ref[head, rows], state, preferred_element_type=F32)
            scale = lax.rsqrt(jnp.mean(num * num, axis=-1, keepdims=True) + 1e-6)
            out_ref[span(step, chunk), cols] = (num * scale).astype(BF16)


def mix_kernel(first, tile, mine_ref, own_ref, other_ref, w_ref, *rest):
    out_ref, stage, sems = rest[-3:]
    rows, depth = own_ref.shape
    mine = mine_ref[0]
    own_rows = pl.ds(pl.multiple_of(mine * depth, depth), depth)
    other_rows = pl.ds(pl.multiple_of((1 - mine) * depth, depth), depth)
    copies = []
    for n in range(stage.shape[1] // tile):
        cols = pl.ds(n * tile, tile)
        total = jnp.dot(own_ref[...], w_ref[own_rows, cols], preferred_element_type=F32)
        total += jnp.dot(other_ref[...], w_ref[other_rows, cols], preferred_element_type=F32)
        stage[:, cols] = total.astype(BF16)
        copies.append(
            pltpu.make_async_copy(stage.at[:, cols], out_ref.at[pl.ds(first, rows), cols], sems.at[n])
        )
        copies[-1].start()
    for copy in copies:
        copy.wait()


def params(mib):
    return pltpu.CompilerParams(vmem_limit_bytes=mib << 20)


def project(x, w_query, w_key, value_weight, chunk):
    rows, depth = x.shape
    heads = value_weight.shape[1] // DV
    steps = rows // chunk
    count = feature_count()
    width = heads * DK
    return pl.pallas_call(
        functools.partial(project_kernel, heads, chunk),
        in_specs=[HBM] * 4,
        out_specs=[VMEM] * 5,
        out_shape=[
            jax.ShapeDtypeStruct((rows, width), BF16),
            jax.ShapeDtypeStruct((width, rows), BF16),
            jax.ShapeDtypeStruct((rows, heads * DV), BF16),
            jax.ShapeDtypeStruct((max(steps - 1, 1), heads, count, DV), F32),
            jax.ShapeDtypeStruct((heads, count, DV), BF16),
        ],
        scratch_shapes=[
            pltpu.VMEM((rows, depth), BF16),
            pltpu.VMEM((depth, width), BF16),
            pltpu.VMEM((depth, width), BF16),
            pltpu.VMEM((depth, heads * DV), BF16),
            pltpu.SemaphoreType.DMA((2 + steps + heads,)),
        ],
        compiler_params=params(20),
        cost_estimate=pl.CostEstimate(
            flops=2 * rows * depth * heads * (DV + 2 * DK), bytes_accessed=12 << 20, transcendentals=0
        ),
        name="project",
    )(in_hbm(x), in_hbm(w_query), in_hbm(w_key), in_hbm(value_weight))


def local_part(q, kt, v, w_out, chunk):
    rows, width = q.shape
    heads = width // DK
    count = feature_count()
    return pl.pallas_call(
        functools.partial(local_kernel, heads, chunk),
        in_specs=[VMEM] * 3 + [HBM],
        out_specs=[VMEM] * 3,
        out_shape=[
            jax.ShapeDtypeStruct((rows, heads * DV), F32),
            jax.ShapeDtypeStruct((heads, rows, count), BF16),
            jax.ShapeDtypeStruct(w_out.shape, BF16),
        ],
        scratch_shapes=[pltpu.SemaphoreType.DMA],
        compiler_params=params(4),
        cost_estimate=pl.CostEstimate(
            flops=8 * rows * chunk * heads * DV, bytes_accessed=8 << 20, transcendentals=0
        ),
        name="local",
    )(q, kt, v, in_hbm(w_out))


def carry(num, phi, before, prefix, chunk, first, rows):
    heads, _, count = phi.shape
    return pl.pallas_call(
        functools.partial(carry_kernel, heads, chunk, first),
        in_specs=[VMEM] * 4,
        out_specs=VMEM,
        out_shape=jax.ShapeDtypeStruct((rows, heads * DV), BF16),
        compiler_params=params(4),
        cost_estimate=pl.CostEstimate(
            flops=2 * rows * count * heads * DV, bytes_accessed=4 << 20, transcendentals=0
        ),
        name="carry",
    )(num, phi, before, prefix)


def mix_pair(mine, own, other, w_out, first, total_rows, earlier):
    rows, depth = own.shape
    width = w_out.shape[1]
    tile = 256 if width % 256 == 0 else width
    operands = [mine, own, other, w_out]
    specs = [SMEM, VMEM, VMEM, VMEM]
    aliases = {}
    if earlier is not None:
        operands.append(earlier)
        specs.append(HBM)
        aliases = {4: 0}
    return pl.pallas_call(
        functools.partial(mix_kernel, first, tile),
        in_specs=specs,
        out_specs=HBM,
        out_shape=jax.ShapeDtypeStruct((total_rows, width), BF16),
        scratch_shapes=[pltpu.VMEM((rows, width), BF16), pltpu.SemaphoreType.DMA((width // tile,))],
        input_output_aliases=aliases,
        compiler_params=params(6),
        cost_estimate=pl.CostEstimate(
            flops=4 * rows * depth * width, bytes_accessed=6 << 20, transcendentals=0
        ),
        name="mix",
    )(*operands)


def swap(value, axis, size, bit):
    return lax.ppermute(value, axis, [(i, i ^ bit) for i in range(size)])


def prefix_of(total, index, odd, upper, size, beside):
    if size == 1:
        return jnp.zeros_like(total), beside
    if size == 4:
        half = total.shape[0] // 2
        low, high = total[:half], total[half:]
        zero = jnp.zeros_like(low)
        got = swap(jnp.where(odd, low, high), "seq", size, 1)
        pair = (jnp.where(odd, high, low).astype(F32) + got.astype(F32)).astype(BF16)
        across = jnp.where(upper, swap(pair, "seq", size, 2), zero)
        send = (across.astype(F32) + jnp.where(odd, zero, low).astype(F32)).astype(BF16)
        send, beside = lax.optimization_barrier((send, beside))
        last = swap(send, "seq", size, 1)
        first = jnp.where(odd, last, across)
        second = jnp.where(odd, got.astype(F32) + across.astype(F32), last.astype(F32)).astype(BF16)
        return jnp.concatenate([first, second], axis=0), beside
    prefix = jnp.zeros(total.shape, F32)
    if size & (size - 1) == 0:
        running = total.astype(F32)
        bit = 1
        while bit < size:
            got = swap(running.astype(BF16), "seq", size, bit).astype(F32)
            prefix = prefix + jnp.where((index & bit) != 0, got, jnp.zeros_like(got))
            running = running + got
            bit *= 2
        return prefix.astype(BF16), beside
    moved = total
    for hop in range(1, size):
        moved = lax.ppermute(moved, "seq", [(i, (i + 1) % size) for i in range(size)])
        prefix = prefix + jnp.where(index >= hop, moved.astype(F32), 0.0)
    return prefix.astype(BF16), beside


def local(seq_size, feat_size, tokens, w_query, w_key, value_weight, w_out):
    rows = tokens.shape[0]
    chunk = 256 if rows % 256 == 0 else rows
    index = lax.axis_index("seq")
    mine = lax.axis_index("feat").astype(jnp.int32).reshape(1)
    place = (tokens, index, (index & 1) == 1, index >= 2, mine)
    tokens, index, odd, upper, mine = lax.optimization_barrier(place)
    q, kt, v, before, total = project(tokens, w_query, w_key, value_weight, chunk)
    num, phi, weight = local_part(q, kt, v, w_out, chunk)
    prefix, (num, phi, weight) = prefix_of(total, index, odd, upper, seq_size, (num, phi, weight))
    if feat_size == 2:
        parts = 2 if rows % (2 * chunk) == 0 else 1
        piece = rows // parts
        out = None
        for part in range(parts):
            normed = carry(num, phi, before, prefix, chunk, part * piece // chunk, piece)
            other = swap(normed, "feat", 2, 1)
            out = mix_pair(mine, normed, other, weight, part * piece, rows, out)
        return out
    normed = carry(num, phi, before, prefix, chunk, 0, rows)
    full = lax.all_gather(normed, "feat", axis=1, tiled=True) if feat_size > 1 else normed
    return jnp.dot(full, weight, preferred_element_type=F32).astype(BF16)


def solution(mesh):
    placed = (
        P(("dp", "seq"), None),
        P(None, "feat"),
        P(None, "feat"),
        P(None, "feat"),
        P(None, "feat"),
    )
    body = functools.partial(local, mesh.shape["seq"], mesh.shape["feat"])
    return jax.shard_map(
        body, mesh=mesh, in_specs=placed, out_specs=P(("dp", "seq"), "feat"), check_vma=False
    )
```

time: 66.6 us -> 43.1 us (0.65)
  the two profiles are of different devices: /device:TPU:19 before, /device:TPU:0 now
where the time goes in v2:
time: 43.1 us; the launch traced here: 43 us
  Pallas kernels  21 us (49%)
  waiting for transfers between devices  14.3 us (33%)
  starting transfers between devices  7.24 us (17%)
    ppermute x5, waiting for transfers between devices, swap(): return lax.ppermute(value, axis, [(i, i ^ bit) for i in range(size)])  14.3 us
    pallas_call x1, Pallas kernels, project(): pl.pallas_call(functools.partial(project_kernel, heads, chunk), in_specs=...  10.1 us
    ppermute x5, starting transfers between devices, swap(): return lax.ppermute(value, axis, [(i, i ^ bit) for i in range(size)])  7.24 us
    pallas_call x2, Pallas kernels, mix_pair(): pl.pallas_call(functools.partial(mix_kernel, first, tile), in_specs=specs...  6.45 us
    pallas_call x1, Pallas kernels, local_part(): pl.pallas_call(functools.partial(local_kernel, heads, chunk), in_specs=[V...  2.81 us
    pallas_call x2, Pallas kernels, carry(): pl.pallas_call(functools.partial(carry_kernel, heads, chunk, first), in_s...  1.67 us
  transfers between devices with their start and end apart: 5, of which 4 were waited for; matrix products, arithmetic and copies ran while one was open for 0% of the time, Pallas kernels for 16%

profile of v2, /device:TPU:0, one launch (start us, length us, event | category | flops | bytes accessed | tf_op | source)
XLA Modules:
  0.0 43.0 jit_solution(7400148606896806333)
XLA Ops:
  0.0 10.1 %project.1 = (bf16[1024,128]{1,0:T(8,128)(2,1)S(1)}, bf16[128,1024]{1,0:T(8,128)(2,1)S(1)}, bf16[1024,1024]{1,0:T(8,128)(2,1)S(1)}, f32[3,8,160,128]{3,2,1,0:T(8,128)S(1)}, bf16[8,160,128]{2,1,0:T(8,128)(2,1)S(1)}) custom-call(bf16[1024,2048]{1,0:T(8,128)(2,1)} %x_in, bf16[2048,128]{1,0:T(8,128)(2,1)} %wq_in.1, bf16[2048,128]{1,0:T(8,128)(2,1)} %wk_in.1, ...), custom_call_target="tpu_custom_call" | custom-call | flops 5368709120 | bytes 12582912 | tf_op jit(solution)/shard_map/project/pallas_call | solution.py:200
  10.1 3.1 %collective-permute-start = (bf16[4,160,128]{2,1,0:T(8,128)(2,1)S(1)}, bf16[4,160,128]{2,1,0:T(8,128)(2,1)S(1)}, u32[]{:S(2)}, u32[]{:S(2)}) collective-permute-start(bf16[4,160,128]{2,1,0:T(8,128)(2,1)S(1)} %broadcast_select_fusion.1), channel_id=1, source_target_pairs={{0,2},{2,0},{4,6},{6,4},{1,3},{3,1},{5,7},{7,5},{8,10},{10,8},{12,... | collective-permute-start | bytes 491528 | tf_op jit(solution)/shard_map/ppermute | solution.py:290
  13.3 4.2 %collective-permute-done = bf16[4,160,128]{2,1,0:T(8,128)(2,1)S(1)} collective-permute-done((bf16[4,160,128]{2,1,0:T(8,128)(2,1)S(1)}, bf16[4,160,128]{2,1,0:T(8,128)(2,1)S(1)}, u32[]{:S(2)}, u32[]{:S(2)}) %collective-permute-start) | collective-permute-done | bytes 163872 | tf_op jit(solution)/shard_map/ppermute | solution.py:290
  17.5 0.1 fusion
  17.5 2.8 %collective-permute-start.1 = (bf16[4,160,128]{2,1,0:T(8,128)(2,1)S(1)}, bf16[4,160,128]{2,1,0:T(8,128)(2,1)S(1)}, u32[]{:S(2)}, u32[]{:S(2)}) collective-permute-start(bf16[4,160,128]{2,1,0:T(8,128)(2,1)S(1)} %fusion), channel_id=1, source_target_pairs={{0,4},{2,6},{4,0},{6,2},{1,5},{3,7},{5,1},{7,3},{8,12},{10,14},{12... | collective-permute-start | bytes 491528 | tf_op jit(solution)/shard_map/ppermute | solution.py:290
  20.4 2.8 %local.1 = (f32[1024,1024]{1,0:T(8,128)S(1)}, bf16[8,1024,160]{2,1,0:T(8,128)(2,1)S(1)}, bf16[2048,1024]{1,0:T(8,128)(2,1)S(1)}) custom-call(bf16[1024,128]{1,0:T(8,128)(2,1)S(1)} %get-tuple-element.26.q_ref, bf16[128,1024]{1,0:T(8,128)(2,1)S(1)} %get-tuple-element.27.kt_ref, bf16[1024,1024]{1,0:T(8,128)(2,1)S(1)} %get-tuple-element.28.v_ref, ...), custom_call_target="tpu_custom_call" | custom-call | flops 2147483648 | bytes 8388608 | tf_op jit(solution)/shard_map/local/pallas_call | solution.py:230
  23.2 4.2 %collective-permute-done.1 = bf16[4,160,128]{2,1,0:T(8,128)(2,1)S(1)} collective-permute-done((bf16[4,160,128]{2,1,0:T(8,128)(2,1)S(1)}, bf16[4,160,128]{2,1,0:T(8,128)(2,1)S(1)}, u32[]{:S(2)}, u32[]{:S(2)}) %collective-permute-start.1) | collective-permute-done | bytes 163872 | tf_op jit(solution)/shard_map/ppermute | solution.py:290
  27.3 0.1 fusion.1
  27.4 0.6 %collective-permute-start.2 = (bf16[4,160,128]{2,1,0:T(8,128)(2,1)S(1)}, bf16[4,160,128]{2,1,0:T(8,128)(2,1)S(1)}, u32[]{:S(2)}, u32[]{:S(2)}) collective-permute-start(bf16[4,160,128]{2,1,0:T(8,128)(2,1)S(1)} %fusion.1), channel_id=1, source_target_pairs={{0,2},{2,0},{4,6},{6,4},{1,3},{3,1},{5,7},{7,5},{8,10},{10,8},{12,... | collective-permute-start | bytes 491528 | tf_op jit(solution)/shard_map/ppermute | solution.py:290
  28.1 4.7 %collective-permute-done.2 = bf16[4,160,128]{2,1,0:T(8,128)(2,1)S(1)} collective-permute-done((bf16[4,160,128]{2,1,0:T(8,128)(2,1)S(1)}, bf16[4,160,128]{2,1,0:T(8,128)(2,1)S(1)}, u32[]{:S(2)}, u32[]{:S(2)}) %collective-permute-start.2) | collective-permute-done | bytes 163872 | tf_op jit(solution)/shard_map/ppermute | solution.py:290
  32.8 0.1 fusion.3
  33.0 0.8 %carry.3.own_ref = bf16[512,1024]{1,0:T(8,128)(2,1)S(1)} custom-call(f32[1024,1024]{1,0:T(8,128)S(1)} %get-tuple-element.32.num_ref, bf16[8,1024,160]{2,1,0:T(8,128)(2,1)S(1)} %get-tuple-element.33.phi_ref, f32[3,8,160,128]{3,2,1,0:T(8,128)S(1)} %get-tuple-element.34.before_ref, bf16[8,160,128]{2,1,0:T(8,128)(2,1)S(1)} %pad_maximum_fusion.prefix_ref), custom_call_target="tpu_custom_call" | custom-call | flops 167772160 | bytes 4194304 | tf_op jit(solution)/shard_map/carry/pallas_call | solution.py:250
  33.8 0.1 collective-permute-start.4
  33.9 0.8 %carry.2.own_ref = bf16[512,1024]{1,0:T(8,128)(2,1)S(1)} custom-call(f32[1024,1024]{1,0:T(8,128)S(1)} %get-tuple-element.32.num_ref, bf16[8,1024,160]{2,1,0:T(8,128)(2,1)S(1)} %get-tuple-element.33.phi_ref, f32[3,8,160,128]{3,2,1,0:T(8,128)S(1)} %get-tuple-element.34.before_ref, bf16[8,160,128]{2,1,0:T(8,128)(2,1)S(1)} %pad_maximum_fusion.prefix_ref), custom_call_target="tpu_custom_call" | custom-call | flops 167772160 | bytes 4194304 | tf_op jit(solution)/shard_map/carry/pallas_call | solution.py:250
  34.7 0.6 %collective-permute-start.3 = (bf16[512,1024]{1,0:T(8,128)(2,1)S(1)}, bf16[512,1024]{1,0:T(8,128)(2,1)S(1)}, u32[]{:S(2)}, u32[]{:S(2)}) collective-permute-start(bf16[512,1024]{1,0:T(8,128)(2,1)S(1)} %carry.2.own_ref), channel_id=1, source_target_pairs={{0,1},{1,0},{2,3},{3,2},{4,5},{5,4},{6,7},{7,6},{8,9},{9,8},{10,11... | collective-permute-start | bytes 3145736 | tf_op jit(solution)/shard_map/ppermute | solution.py:290
  35.3 1.2 %collective-permute-done.4.other_ref = bf16[512,1024]{1,0:T(8,128)(2,1)S(1)} collective-permute-done((bf16[512,1024]{1,0:T(8,128)(2,1)S(1)}, bf16[512,1024]{1,0:T(8,128)(2,1)S(1)}, u32[]{:S(2)}, u32[]{:S(2)}) %collective-permute-start.4) | collective-permute-done | bytes 1048608 | tf_op jit(solution)/shard_map/ppermute | solution.py:290
  36.5 3.2 %mix.2.rest_0_ = bf16[1024,1024]{1,0:T(8,128)(2,1)} custom-call(s32[1]{0:T(128)} %bitcast.mine_ref, bf16[512,1024]{1,0:T(8,128)(2,1)S(1)} %carry.3.own_ref, bf16[512,1024]{1,0:T(8,128)(2,1)S(1)} %collective-permute-done.4.other_ref, bf16[2048,1024]{1,0:T(8,128)(2,1)S(1)} %get-tuple-element.36.w_ref), custom_call_target="tpu_custom_call" | custom-call | flops 2147483648 | bytes 6291456 | tf_op jit(solution)/shard_map/mix/pallas_call | solution.py:274
  39.8 0.0 collective-permute-done.3.other_ref
  39.8 3.2 %mix.3 = bf16[1024,1024]{1,0:T(8,128)(2,1)} custom-call(s32[1]{0:T(128)} %bitcast.mine_ref, bf16[512,1024]{1,0:T(8,128)(2,1)S(1)} %carry.2.own_ref, bf16[512,1024]{1,0:T(8,128)(2,1)S(1)} %collective-permute-done.3.other_ref, bf16[2048,1024]{1,0:T(8,128)(2,1)S(1)} %get-tuple-element.36.w_ref, ...), custom_call_target="tpu_custom_call", output_to_operand_aliasing={{}: (4, {})} | custom-call | flops 2147483648 | bytes 6291456 | tf_op jit(solution)/shard_map/mix/pallas_call | solution.py:274
  (3 shorter events, 0.1 us)
Async XLA Ops:
  10.1 7.3 %collective-permute-start = (bf16[4,160,128]{2,1,0:T(8,128)(2,1)S(1)}, bf16[4,160,128]{2,1,0:T(8,128)(2,1)S(1)}, u32[]{:S(2)}, u32[]{:S(2)}) collective-permute-start(bf16[4,160,128]{2,1,0:T(8,128)(2,1)S(1)} %broadcast_select_fusion.1), channel_id=1, source_target_pairs={{0,2},{2,0},{4,6},{6,4},{1,3},{3,1},{5,7},{7,5},{8,10},{10,8},{12,... | collective-permute-start | bytes 491528 | tf_op jit(solution)/shard_map/ppermute | solution.py:290
  17.5 9.8 %collective-permute-start.1 = (bf16[4,160,128]{2,1,0:T(8,128)(2,1)S(1)}, bf16[4,160,128]{2,1,0:T(8,128)(2,1)S(1)}, u32[]{:S(2)}, u32[]{:S(2)}) collective-permute-start(bf16[4,160,128]{2,1,0:T(8,128)(2,1)S(1)} %fusion), channel_id=1, source_target_pairs={{0,4},{2,6},{4,0},{6,2},{1,5},{3,7},{5,1},{7,3},{8,12},{10,14},{12... | collective-permute-start | bytes 491528 | tf_op jit(solution)/shard_map/ppermute | solution.py:290
  27.4 5.4 %collective-permute-start.2 = (bf16[4,160,128]{2,1,0:T(8,128)(2,1)S(1)}, bf16[4,160,128]{2,1,0:T(8,128)(2,1)S(1)}, u32[]{:S(2)}, u32[]{:S(2)}) collective-permute-start(bf16[4,160,128]{2,1,0:T(8,128)(2,1)S(1)} %fusion.1), channel_id=1, source_target_pairs={{0,2},{2,0},{4,6},{6,4},{1,3},{3,1},{5,7},{7,5},{8,10},{10,8},{12,... | collective-permute-start | bytes 491528 | tf_op jit(solution)/shard_map/ppermute | solution.py:290
  33.8 2.7 %collective-permute-start.4 = (bf16[512,1024]{1,0:T(8,128)(2,1)S(1)}, bf16[512,1024]{1,0:T(8,128)(2,1)S(1)}, u32[]{:S(2)}, u32[]{:S(2)}) collective-permute-start(bf16[512,1024]{1,0:T(8,128)(2,1)S(1)} %carry.3.own_ref), channel_id=1, source_target_pairs={{0,1},{1,0},{2,3},{3,2},{4,5},{5,4},{6,7},{7,6},{8,9},{9,8},{10,11... | collective-permute-start | bytes 3145736 | tf_op jit(solution)/shard_map/ppermute | solution.py:290
  34.7 5.0 %collective-permute-start.3 = (bf16[512,1024]{1,0:T(8,128)(2,1)S(1)}, bf16[512,1024]{1,0:T(8,128)(2,1)S(1)}, u32[]{:S(2)}, u32[]{:S(2)}) collective-permute-start(bf16[512,1024]{1,0:T(8,128)(2,1)S(1)} %carry.2.own_ref), channel_id=1, source_target_pairs={{0,1},{1,0},{2,3},{3,2},{4,5},{5,4},{6,7},{7,6},{8,9},{9,8},{10,11... | collective-permute-start | bytes 3145736 | tf_op jit(solution)/shard_map/ppermute | solution.py:290

commit v3 on v2

v3 whole, which is shorter than its diff:
```python
import functools

import jax
import jax.numpy as jnp
from jax import lax
from jax.experimental import pallas as pl
from jax.experimental.pallas import tpu as pltpu
from jax.sharding import PartitionSpec as P

DK = 16
DV = 128
F32 = jnp.float32
BF16 = jnp.bfloat16


def feature_tiles(rows, linear, square, cross):
    half = DK // 2
    tiles = [rows * linear if linear != 1.0 else rows]
    for shift in range(half):
        other = rows if shift == 0 else pltpu.roll(rows, shift, 0)
        weight = square if shift == 0 else cross
        product = rows * other
        tiles.append(product * weight if weight != 1.0 else product)
    far = rows[:half] * rows[half:]
    one = (lax.broadcasted_iota(jnp.int32, far.shape, 0) == 0).astype(F32)
    tiles.append(jnp.concatenate([far * cross if cross != 1.0 else far, one], axis=0))
    return jnp.concatenate([tile.astype(BF16) for tile in tiles], axis=0)


def feature_count():
    return DK + (DK // 2) * DK + DK


VMEM = pl.BlockSpec(memory_space=pltpu.VMEM)
HBM = pl.BlockSpec(memory_space=pltpu.HBM)
SMEM = pl.BlockSpec(memory_space=pltpu.SMEM)


def in_hbm(value):
    return pltpu.with_memory_space_constraint(value, pltpu.HBM)


def span(index, size):
    return slice(index * size, (index + 1) * size)


def halves(count):
    middle = max(count // 2, 1)
    return range(middle), range(middle, count)


def project_kernel(heads, rest, chunk, *refs):
    x_in, wq_in, wk_in, wv_in, q_ref, kt_ref, v_ref, before_ref, total_ref, x_ref = refs[:10]
    later_ref = refs[10] if rest else None
    wq_ref, wk_ref, wv_ref, sems = refs[-4:]
    steps = x_in.shape[0] // chunk
    width = kt_ref.shape[0]
    group = 2 if heads % 2 == 0 else 1
    groups = heads // group
    cols = group * DV
    copies = {}

    def fetch(key, source, target):
        copies[key] = pltpu.make_async_copy(source, target, sems.at[len(copies)])
        copies[key].start()

    def fetch_x(m):
        rows = pl.ds(m * chunk, chunk)
        fetch(("x", m), x_in.at[rows], x_ref.at[rows])

    def wait(keys):
        for key in keys:
            copies[key].wait()

    def project_qk(m):
        rows = span(m, chunk)
        both = jnp.concatenate([wq_ref[...], wk_ref[...]], axis=1)
        qk = jnp.dot(x_ref[rows, :], both, preferred_element_type=F32)
        q_ref[rows, :] = qk[:, :width].astype(BF16)
        kt_ref[:, rows] = qk[:, width:].T.astype(BF16)

    project_v = ValueSteps(0, group, chunk, steps, x_ref, wv_ref, kt_ref, v_ref, before_ref, total_ref)
    early, late = halves(steps)
    fetch("q", wq_in, wq_ref)
    fetch("k", wk_in, wk_ref)
    for m in early:
        fetch_x(m)
    for g in range(groups):
        pair = pl.ds(g * cols, cols)
        fetch(("v", g), wv_in.at[:, pair], wv_ref.at[:, pair])
    for m in late:
        fetch_x(m)
    if rest:
        fetch("later", wv_in.at[:, pl.ds(heads * DV, rest * DV)], later_ref)
    wait(["q", "k"] + [("x", m) for m in early])
    for m in early:
        project_qk(m)
    wait([("v", g) for g in range(groups)])
    for m in early:
        for g in range(groups):
            project_v(m, g)
    wait([("x", m) for m in late])
    for m in late:
        project_qk(m)
        for g in range(groups):
            project_v(m, g)
    project_v.finish()
    if rest:
        wait(["later"])


class ValueSteps:
    def __init__(self, first, group, chunk, steps, x_ref, wv_ref, kt_ref, v_ref, before_ref, total_ref):
        self.first, self.group, self.chunk, self.steps = first, group, chunk, steps
        self.x_ref, self.wv_ref, self.kt_ref, self.v_ref = x_ref, wv_ref, kt_ref, v_ref
        self.before_ref, self.total_ref = before_ref, total_ref
        self.pending = []

    def __call__(self, m, g):
        rows, cols = span(m, self.chunk), span(g, self.group * DV)
        self.v_ref[rows, cols] = jnp.dot(
            self.x_ref[rows, :], self.wv_ref[:, cols], preferred_element_type=F32
        ).astype(BF16)
        self.pending.append((m, g))
        if len(self.pending) > 1:
            self.add_states(*self.pending.pop(0))

    def finish(self):
        for item in self.pending:
            self.add_states(*item)

    def add_states(self, m, g):
        rows = span(m, self.chunk)
        for head in range(g * self.group, (g + 1) * self.group):
            keys = self.kt_ref[span(self.first + head, DK), rows].astype(F32)
            phi = feature_tiles(keys, 1.0, 1.0, 1.0)
            new = jnp.dot(phi, self.v_ref[rows, span(head, DV)], preferred_element_type=F32)
            if m > 0:
                new = self.before_ref[m - 1, head] + new
            if m < self.steps - 1:
                self.before_ref[m, head] = new
            else:
                self.total_ref[head] = new.astype(BF16)


def project_later_kernel(first, heads, chunk, x_ref, wv_ref, kt_ref, w_in, v_ref, before_ref, total_ref, w_ref, sem):
    fetch = pltpu.make_async_copy(w_in, w_ref, sem)
    fetch.start()
    steps = x_ref.shape[0] // chunk
    group = 2 if heads % 2 == 0 else 1
    project_v = ValueSteps(first, group, chunk, steps, x_ref, wv_ref, kt_ref, v_ref, before_ref, total_ref)
    for m in range(steps):
        for g in range(heads // group):
            project_v(m, g)
    project_v.finish()
    fetch.wait()


def local_kernel(first, heads, chunk, q_ref, kt_ref, v_ref, num_ref, phi_ref):
    causal = lax.broadcasted_iota(jnp.int32, (chunk, chunk), 0) >= lax.broadcasted_iota(
        jnp.int32, (chunk, chunk), 1
    )
    owner = lax.broadcasted_iota(jnp.int32, (kt_ref.shape[0], chunk), 0) // DK
    for m in range(q_ref.shape[0] // chunk):
        rows = span(m, chunk)
        kt = kt_ref[:, rows]
        q = q_ref[rows, :].astype(F32)
        qt = q.T
        quarter = (q * 0.25).astype(BF16)
        for head in range(heads):
            keys = jnp.where(owner == first + head, kt, jnp.zeros_like(kt))
            s = jnp.dot(quarter, keys, preferred_element_type=F32)
            w = jnp.where(causal, 1.0 + s * (1.0 + 0.5 * s), 0.0).astype(BF16)
            cols = span(head, DV)
            num_ref[rows, cols] = jnp.dot(w, v_ref[rows, cols], preferred_element_type=F32)
            phi = feature_tiles(qt[span(first + head, DK)], 0.25, 1.0 / 32.0, 1.0 / 16.0)
            phi_ref[head, rows] = phi.T


def carry_kernel(heads, chunk, num_ref, phi_ref, before_ref, prefix_ref, out_ref):
    for m in range(out_ref.shape[0] // chunk):
        rows = span(m, chunk)
        for head in range(heads):
            cols = span(head, DV)
            state = prefix_ref[head]
            if m > 0:
                state = (state.astype(F32) + before_ref[m - 1, head]).astype(BF16)
            num = num_ref[rows, cols] + jnp.dot(phi_ref[head, rows], state, preferred_element_type=F32)
            scale = lax.rsqrt(jnp.mean(num * num, axis=-1, keepdims=True) + 1e-6)
            out_ref[rows, cols] = (num * scale).astype(BF16)


def weight_rows(mine, owner, offset, depth, w_ref):
    half = w_ref.shape[0] // 2
    start = jnp.where(owner == 0, mine, 1 - mine) * half + offset
    return pl.ds(pl.multiple_of(start, depth), depth)


def mix_kernel(offset, terms, tile, chained, final, mine_ref, w_ref, *refs):
    values, refs = refs[: len(terms)], refs[len(terms) :]
    running = refs[0] if chained else None
    out_ref = refs[1] if chained else refs[0]
    rows, depth = values[0].shape
    mine = mine_ref[0]
    copies = []
    for n in range(w_ref.shape[1] // tile):
        cols = pl.ds(n * tile, tile)
        total = running[:, cols] if chained else None
        for owner, value in zip(terms, values):
            product = jnp.dot(
                value[...], w_ref[weight_rows(mine, owner, offset, depth, w_ref), cols], preferred_element_type=F32
            )
            total = product if total is None else total + product
        if not final:
            out_ref[:, cols] = total
            continue
        stage, sems = refs[-2:]
        stage[:, cols] = total.astype(BF16)
        copies.append(pltpu.make_async_copy(stage.at[:, cols], out_ref.at[:, cols], sems.at[n]))
        copies[-1].start()
    for copy in copies:
        copy.wait()


def params(mib):
    return pltpu.CompilerParams(vmem_limit_bytes=mib << 20)


def cost(flops, mib):
    return pl.CostEstimate(flops=flops, bytes_accessed=mib << 20, transcendentals=0)


def project(x, w_query, w_key, value_weight, heads, chunk):
    rows, depth = x.shape
    rest = value_weight.shape[1] // DV - heads
    steps = rows // chunk
    count = feature_count()
    width = w_query.shape[1]
    shapes = [
        jax.ShapeDtypeStruct((rows, width), BF16),
        jax.ShapeDtypeStruct((width, rows), BF16),
        jax.ShapeDtypeStruct((rows, heads * DV), BF16),
        jax.ShapeDtypeStruct((max(steps - 1, 1), heads, count, DV), F32),
        jax.ShapeDtypeStruct((heads, count, DV), BF16),
        jax.ShapeDtypeStruct((rows, depth), BF16),
    ]
    if rest:
        shapes.append(jax.ShapeDtypeStruct((depth, rest * DV), BF16))
    return pl.pallas_call(
        functools.partial(project_kernel, heads, rest, chunk),
        in_specs=[HBM] * 4,
        out_specs=[VMEM] * len(shapes),
        out_shape=shapes,
        scratch_shapes=[
            pltpu.VMEM((depth, width), BF16),
            pltpu.VMEM((depth, width), BF16),
            pltpu.VMEM((depth, heads * DV), BF16),
            pltpu.SemaphoreType.DMA((3 + steps + heads,)),
        ],
        compiler_params=params(12),
        cost_estimate=cost(2 * rows * depth * (heads * DV + 2 * width), 12),
        name="project",
    )(in_hbm(x), in_hbm(w_query), in_hbm(w_key), in_hbm(value_weight))


def project_later(x, weight, kt, w_out, first, chunk):
    rows, depth = x.shape
    heads = weight.shape[1] // DV
    steps = rows // chunk
    count = feature_count()
    return pl.pallas_call(
        functools.partial(project_later_kernel, first, heads, chunk),
        in_specs=[VMEM] * 3 + [HBM],
        out_specs=[VMEM] * 4,
        out_shape=[
            jax.ShapeDtypeStruct((rows, heads * DV), BF16),
            jax.ShapeDtypeStruct((max(steps - 1, 1), heads, count, DV), F32),
            jax.ShapeDtypeStruct((heads, count, DV), BF16),
            jax.ShapeDtypeStruct(w_out.shape, BF16),
        ],
        scratch_shapes=[pltpu.SemaphoreType.DMA],
        compiler_params=params(4),
        cost_estimate=cost(2 * rows * depth * heads * DV, 8),
        name="project_later",
    )(x, weight, kt, in_hbm(w_out))


def local_part(q, kt, v, first, chunk):
    rows = q.shape[0]
    heads = v.shape[1] // DV
    count = feature_count()
    return pl.pallas_call(
        functools.partial(local_kernel, first, heads, chunk),
        in_specs=[VMEM] * 3,
        out_specs=[VMEM] * 2,
        out_shape=[
            jax.ShapeDtypeStruct((rows, heads * DV), F32),
            jax.ShapeDtypeStruct((heads, rows, count), BF16),
        ],
        compiler_params=params(4),
        cost_estimate=cost(8 * rows * chunk * heads * DV, 4),
        name="local",
    )(q, kt, v)


def carry(num, phi, before, prefix, chunk):
    heads, rows, count = phi.shape
    return pl.pallas_call(
        functools.partial(carry_kernel, heads, chunk),
        in_specs=[VMEM] * 4,
        out_specs=VMEM,
        out_shape=jax.ShapeDtypeStruct((rows, heads * DV), BF16),
        compiler_params=params(4),
        cost_estimate=cost(2 * rows * count * heads * DV, 4),
        name="carry",
    )(num, phi, before, prefix)


def mix(mine, w_out, terms, values, offset, running=None, final=False):
    rows, depth = values[0].shape
    width = w_out.shape[1]
    tile = 256 if width % 256 == 0 else width
    operands = [mine, w_out] + list(values) + ([] if running is None else [running])
    scratch = [pltpu.VMEM((rows, width), BF16), pltpu.SemaphoreType.DMA((width // tile,))]
    return pl.pallas_call(
        functools.partial(mix_kernel, offset, terms, tile, running is not None, final),
        in_specs=[SMEM] + [VMEM] * (len(operands) - 1),
        out_specs=HBM if final else VMEM,
        out_shape=jax.ShapeDtypeStruct((rows, width), BF16 if final else F32),
        scratch_shapes=scratch if final else [],
        compiler_params=params(8),
        cost_estimate=cost(2 * len(terms) * rows * depth * width, 4),
        name="mix",
    )(*operands)


def swap(value, axis, size, bit):
    return lax.ppermute(value, axis, [(i, i ^ bit) for i in range(size)])


def widen(value):
    return value.astype(F32)


class QuadPrefix:
    def __init__(self, total, odd, upper):
        half = total.shape[0] // 2
        self.low, self.high = total[:half], total[half:]
        self.odd, self.upper = odd, upper
        self.zero = jnp.zeros_like(self.low)

    def send_first(self):
        return jnp.where(self.odd, self.low, self.high)

    def send_second(self, first):
        self.first = first
        return (jnp.where(self.odd, widen(self.high), widen(self.low)) + widen(first)).astype(BF16)

    def send_third(self, second):
        self.across = jnp.where(self.upper, second, self.zero)
        return (widen(self.across) + jnp.where(self.odd, 0.0, widen(self.low))).astype(BF16)

    def finish(self, third):
        low = jnp.where(self.odd, third, self.across)
        high = jnp.where(self.odd, widen(self.first) + widen(self.across), widen(third)).astype(BF16)
        return jnp.concatenate([low, high], axis=0)


def any_prefix(total, index, size):
    if size == 1:
        return jnp.zeros_like(total)
    prefix = jnp.zeros(total.shape, F32)
    if size & (size - 1) == 0:
        running = widen(total)
        bit = 1
        while bit < size:
            got = widen(swap(running.astype(BF16), "seq", size, bit))
            prefix = prefix + jnp.where((index & bit) != 0, got, 0.0)
            running = running + got
            bit *= 2
        return prefix.astype(BF16)
    moved = total
    for hop in range(1, size):
        moved = lax.ppermute(moved, "seq", [(i, (i + 1) % size) for i in range(size)])
        prefix = prefix + jnp.where(index >= hop, widen(moved), 0.0)
    return prefix.astype(BF16)


def local(seq_size, feat_size, tokens, w_query, w_key, value_weight, w_out):
    rows = tokens.shape[0]
    heads = value_weight.shape[1] // DV
    chunk = 256 if rows % 256 == 0 else rows
    index = lax.axis_index("seq")
    mine = lax.axis_index("feat").astype(jnp.int32).reshape(1)
    place = (tokens, index, (index & 1) == 1, index >= 2, mine)
    tokens, index, odd, upper, mine = lax.optimization_barrier(place)
    if seq_size != 4 or feat_size != 2 or heads % 4 != 0:
        q, kt, v, before, total, _ = project(tokens, w_query, w_key, value_weight, heads, chunk)
        prefix = any_prefix(total, index, seq_size)
        num, phi = local_part(q, kt, v, 0, chunk)
        normed = carry(num, phi, before, prefix, chunk)
        full = lax.all_gather(normed, "feat", axis=1, tiled=True) if feat_size > 1 else normed
        return jnp.dot(full, w_out, preferred_element_type=F32).astype(BF16)

    together = lax.optimization_barrier
    near = functools.partial(swap, axis="seq", size=4, bit=1)
    far = functools.partial(swap, axis="seq", size=4, bit=2)
    twin = functools.partial(swap, axis="feat", size=2, bit=1)
    part = heads // 2
    q, kt, v_a, before_a, total_a, x, later = project(tokens, w_query, w_key, value_weight, part, chunk)
    prefix_a = QuadPrefix(total_a, odd, upper)
    a1 = near(prefix_a.send_first())
    v_b, before_b, total_b, weight = project_later(x, later, kt, w_out, part, chunk)
    prefix_b = QuadPrefix(total_b, odd, upper)
    send_a, send_b, q = together((prefix_a.send_second(a1), prefix_b.send_first(), q))
    a2 = far(send_a)
    b1 = near(send_b)
    num_a, phi_a = local_part(q, kt, v_a, 0, chunk)
    send_b, num_a, phi_a, q = together((prefix_b.send_second(b1), num_a, phi_a, q))
    b2 = far(send_b)
    a3 = near(prefix_a.send_third(a2))
    num_b, phi_b = local_part(q, kt, v_b, part, chunk)
    sum_a, num_b, phi_b = together((prefix_a.finish(a3), num_b, phi_b))
    normed_a = carry(num_a, phi_a, before_a, sum_a, chunk)
    other_a = twin(normed_a)
    send_b, other_a = together((prefix_b.send_third(b2), other_a))
    b3 = near(send_b)
    running = mix(mine, weight, (0, 1), (normed_a, other_a), 0)
    sum_b, running = together((prefix_b.finish(b3), running))
    normed_b = carry(num_b, phi_b, before_b, sum_b, chunk)
    other_b = twin(normed_b)
    running = mix(mine, weight, (0,), (normed_b,), part * DV, running)
    return mix(mine, weight, (1,), (other_b,), part * DV, running, final=True)


def solution(mesh):
    placed = (
        P(("dp", "seq"), None),
        P(None, "feat"),
        P(None, "feat"),
        P(None, "feat"),
        P(None, "feat"),
    )
    body = functools.partial(local, mesh.shape["seq"], mesh.shape["feat"])
    return jax.shard_map(
        body, mesh=mesh, in_specs=placed, out_specs=P(("dp", "seq"), "feat"), check_vma=False
    )
```

time: 43.1 us -> 43.7 us (1.014)
  starting transfers between devices: 7.24 us -> 9.43 us
  waiting for transfers between devices: 14.3 us -> 12.9 us
    ppermute x5 -> x8, starting transfers between devices: 7.24 us -> 9.43 us  [swap(): return lax.ppermute(value, axis, [(i, i ^ bit) for i in range(size)])]
    ppermute x5 -> x8, waiting for transfers between devices: 14.3 us -> 12.9 us  [swap(): return lax.ppermute(value, axis, [(i, i ^ bit) for i in range(size)])]
    pallas_call x6 -> x9, Pallas kernels: 21 us -> 20.7 us  [the longest x1 6.82 us: project(): pl.pallas_call(functools.partial(project_kernel, heads, rest, chunk), in_...]
  transfers between devices with their start and end apart: 5 -> 8, of which waited for: 4 -> 6; matrix products, arithmetic and copies ran while one was open for 0% -> 0% of each run, Pallas kernels for 16% -> 23%
where the time goes in v3:
time: 43.7 us; the launch traced here: 43.5 us
  Pallas kernels  20.7 us (47%)
  waiting for transfers between devices  12.9 us (30%)
  starting transfers between devices  9.43 us (22%)
    ppermute x8, waiting for transfers between devices, swap(): return lax.ppermute(value, axis, [(i, i ^ bit) for i in range(size)])  12.9 us
    ppermute x8, starting transfers between devices, swap(): return lax.ppermute(value, axis, [(i, i ^ bit) for i in range(size)])  9.43 us
    pallas_call x1, Pallas kernels, project(): pl.pallas_call(functools.partial(project_kernel, heads, rest, chunk), in_...  6.82 us
    pallas_call x3, Pallas kernels, mix(): pl.pallas_call(functools.partial(mix_kernel, offset, terms, tile, running...  5.95 us
    pallas_call x1, Pallas kernels, project_later(): pl.pallas_call(functools.partial(project_later_kernel, first, heads, chun...  3.34 us
    pallas_call x2, Pallas kernels, local_part(): pl.pallas_call(functools.partial(local_kernel, first, heads, chunk), in_s...  2.89 us
    pallas_call x2, Pallas kernels, carry(): pl.pallas_call(functools.partial(carry_kernel, heads, chunk), in_specs=[V...  1.69 us
  transfers between devices with their start and end apart: 8, of which 6 were waited for; matrix products, arithmetic and copies ran while one was open for 0% of the time, Pallas kernels for 23%

profile of v3, /device:TPU:0, one launch (start us, length us, event | category | flops | bytes accessed | tf_op | source)
XLA Modules:
  0.0 43.5 jit_solution(7965361113879644588)
XLA Ops:
  0.0 6.8 %project.1 = (bf16[1024,128]{1,0:T(8,128)(2,1)S(1)}, bf16[128,1024]{1,0:T(8,128)(2,1)S(1)}, bf16[1024,512]{1,0:T(8,128)(2,1)S(1)}, f32[3,4,160,128]{3,2,1,0:T(8,...) custom-call(bf16[1024,2048]{1,0:T(8,128)(2,1)} %refs_0_, ...), custom_call_target="tpu_custom_call" | custom-call | flops 3221225472 | bytes 12582912 | tf_op jit(solution)/shard_map/project/pallas_call | solution.py:249
  6.9 3.1 %collective-permute-start = (bf16[2,160,128]{2,1,0:T(8,128)(2,1)S(1)}, bf16[2,160,128]{2,1,0:T(8,128)(2,1)S(1)}, u32[]{:S(2)}, u32[]{:S(2)}) collective-permute-start(bf16[2,160,128]{2,1,0:T(8,128)(2,1)S(1)} %broadcast_select_fusion.5), channel_id=1, source_target_pairs={{0,2},{2,0},{4,6},{6,4},{1,3},{3,1},{5,7},{7,5},{8,10},{10,8},{12,... | collective-permute-start | bytes 245768 | tf_op jit(solution)/shard_map/ppermute | solution.py:338
  10.0 3.3 %project_later.1 = (bf16[1024,512]{1,0:T(8,128)(2,1)S(1)}, f32[3,4,160,128]{3,2,1,0:T(8,128)S(1)}, bf16[4,160,128]{2,1,0:T(8,128)(2,1)S(1)}, bf16[2048,1024]{1,0:T(8,128)(2,1)S(1)}) custom-call(bf16[1024,2048]{1,0:T(8,128)(2,1)S(1)} %get-tuple-element.40.x_ref, bf16[2048,512]{1,0:T(8,128)(2,1)S(1)} %get-tuple-element.41.wv_ref, ...), custom_call_target="tpu_custom_call" | custom-call | flops 2147483648 | bytes 8388608 | tf_op jit(solution)/shard_map/project_later/pallas_call | solution.py:271
  13.4 2.6 %collective-permute-start.1 = (bf16[2,160,128]{2,1,0:T(8,128)(2,1)S(1)}, bf16[2,160,128]{2,1,0:T(8,128)(2,1)S(1)}, u32[]{:S(2)}, u32[]{:S(2)}) collective-permute-start(bf16[2,160,128]{2,1,0:T(8,128)(2,1)S(1)} %fusion), channel_id=1, source_target_pairs={{0,4},{2,6},{4,0},{6,2},{1,5},{3,7},{5,1},{7,3},{8,12},{10,14},{12... | collective-permute-start | bytes 245768 | tf_op jit(solution)/shard_map/ppermute | solution.py:338
  16.1 1.1 %collective-permute-start.3 = (bf16[2,160,128]{2,1,0:T(8,128)(2,1)S(1)}, bf16[2,160,128]{2,1,0:T(8,128)(2,1)S(1)}, u32[]{:S(2)}, u32[]{:S(2)}) collective-permute-start(bf16[2,160,128]{2,1,0:T(8,128)(2,1)S(1)} %broadcast_select_fusion.4), channel_id=1, source_target_pairs={{0,2},{2,0},{4,6},{6,4},{1,3},{3,1},{5,7},{7,5},{8,10},{10,8},{12,... | collective-permute-start | bytes 245768 | tf_op jit(solution)/shard_map/ppermute | solution.py:338
  17.1 1.4 %local.2 = (f32[1024,512]{1,0:T(8,128)S(1)}, bf16[4,1024,160]{2,1,0:T(8,128)(2,1)S(1)}) custom-call(bf16[1024,128]{1,0:T(8,128)(2,1)S(1)} %get-tuple-element.55.q_ref, bf16[128,1024]{1,0:T(8,128)(2,1)S(1)} %get-tuple-element.42.kt_ref, bf16[1024,512]{1,0:T(8,128)(2,1)S(1)} %get-tuple-element.52.v_ref), custom_call_target="tpu_custom_call" | custom-call | flops 1073741824 | bytes 4194304 | tf_op jit(solution)/shard_map/local/pallas_call | solution.py:292
  18.6 1.3 %collective-permute-done.1 = bf16[2,160,128]{2,1,0:T(8,128)(2,1)S(1)} collective-permute-done((bf16[2,160,128]{2,1,0:T(8,128)(2,1)S(1)}, bf16[2,160,128]{2,1,0:T(8,128)(2,1)S(1)}, u32[]{:S(2)}, u32[]{:S(2)}) %collective-permute-start.1) | collective-permute-done | bytes 81952 | tf_op jit(solution)/shard_map/ppermute | solution.py:338
  19.9 0.3 collective-permute-start.2
  20.2 0.5 %collective-permute-done.3 = bf16[2,160,128]{2,1,0:T(8,128)(2,1)S(1)} collective-permute-done((bf16[2,160,128]{2,1,0:T(8,128)(2,1)S(1)}, bf16[2,160,128]{2,1,0:T(8,128)(2,1)S(1)}, u32[]{:S(2)}, u32[]{:S(2)}) %collective-permute-start.3) | collective-permute-done | bytes 81952 | tf_op jit(solution)/shard_map/ppermute | solution.py:338
  20.8 1.4 %local.3 = (f32[1024,512]{1,0:T(8,128)S(1)}, bf16[4,1024,160]{2,1,0:T(8,128)(2,1)S(1)}) custom-call(bf16[1024,128]{1,0:T(8,128)(2,1)S(1)} %get-tuple-element.55.q_ref, bf16[128,1024]{1,0:T(8,128)(2,1)S(1)} %get-tuple-element.42.kt_ref, bf16[1024,512]{1,0:T(8,128)(2,1)S(1)} %get-tuple-element.56.v_ref), custom_call_target="tpu_custom_call" | custom-call | flops 1073741824 | bytes 4194304 | tf_op jit(solution)/shard_map/local/pallas_call | solution.py:292
  22.2 2.2 %collective-permute-done.2 = bf16[2,160,128]{2,1,0:T(8,128)(2,1)S(1)} collective-permute-done((bf16[2,160,128]{2,1,0:T(8,128)(2,1)S(1)}, bf16[2,160,128]{2,1,0:T(8,128)(2,1)S(1)}, u32[]{:S(2)}, u32[]{:S(2)}) %collective-permute-start.2) | collective-permute-done | bytes 81952 | tf_op jit(solution)/shard_map/ppermute | solution.py:338
  24.5 0.8 %carry.2.refs_0_ = bf16[1024,512]{1,0:T(8,128)(2,1)S(1)} custom-call(f32[1024,512]{1,0:T(8,128)S(1)} %get-tuple-element.63.num_ref, bf16[4,1024,160]{2,1,0:T(8,128)(2,1)S(1)} %get-tuple-element.64.phi_ref, f32[3,4,160,128]{3,2,1,0:T(8,128)S(1)} %get-tuple-element.65.before_ref, bf16[4,160,128]{2,1,0:T(8,128)(2,1)S(1)} %pad_maximum_fusion.prefix_ref), custom_call_target="tpu_custom_call" | custom-call | flops 167772160 | bytes 4194304 | tf_op jit(solution)/shard_map/carry/pallas_call | solution.py:308
  25.4 0.1 collective-permute-start.5
  25.4 2.0 %collective-permute-start.4 = (bf16[2,160,128]{2,1,0:T(8,128)(2,1)S(1)}, bf16[2,160,128]{2,1,0:T(8,128)(2,1)S(1)}, u32[]{:S(2)}, u32[]{:S(2)}) collective-permute-start(bf16[2,160,128]{2,1,0:T(8,128)(2,1)S(1)} %fusion.4), channel_id=1, source_target_pairs={{0,4},{2,6},{4,0},{6,2},{1,5},{3,7},{5,1},{7,3},{8,12},{10,14},{12... | collective-permute-start | bytes 245768 | tf_op jit(solution)/shard_map/ppermute | solution.py:338
  27.5 5.5 %collective-permute-done.4 = bf16[2,160,128]{2,1,0:T(8,128)(2,1)S(1)} collective-permute-done((bf16[2,160,128]{2,1,0:T(8,128)(2,1)S(1)}, bf16[2,160,128]{2,1,0:T(8,128)(2,1)S(1)}, u32[]{:S(2)}, u32[]{:S(2)}) %collective-permute-start.4) | collective-permute-done | bytes 81952 | tf_op jit(solution)/shard_map/ppermute | solution.py:338
  33.0 0.0 collective-permute-done.5.refs_1_
  33.0 0.1 collective-permute-start.6
  33.1 2.3 %mix.3.refs_1_ = f32[1024,1024]{1,0:T(8,128)S(1)} custom-call(s32[1]{0:T(128)} %bitcast.mine_ref, bf16[2048,1024]{1,0:T(8,128)(2,1)S(1)} %get-tuple-element.43.w_ref, bf16[1024,512]{1,0:T(8,128)(2,1)S(1)} %carry.2.refs_0_, bf16[1024,512]{1,0:T(8,128)(2,1)S(1)} %collective-permute-done.5.refs_1_), custom_call_target="tpu_custom_call" | custom-call | flops 2147483648 | bytes 4194304 | tf_op jit(solution)/shard_map/mix/pallas_call | solution.py:325
  35.5 2.1 %collective-permute-done.6 = bf16[2,160,128]{2,1,0:T(8,128)(2,1)S(1)} collective-permute-done((bf16[2,160,128]{2,1,0:T(8,128)(2,1)S(1)}, bf16[2,160,128]{2,1,0:T(8,128)(2,1)S(1)}, u32[]{:S(2)}, u32[]{:S(2)}) %collective-permute-start.6) | collective-permute-done | bytes 81952 | tf_op jit(solution)/shard_map/ppermute | solution.py:338
  37.6 0.8 %carry.3.refs_0_ = bf16[1024,512]{1,0:T(8,128)(2,1)S(1)} custom-call(f32[1024,512]{1,0:T(8,128)S(1)} %get-tuple-element.59.num_ref, bf16[4,1024,160]{2,1,0:T(8,128)(2,1)S(1)} %get-tuple-element.60.phi_ref, f32[3,4,160,128]{3,2,1,0:T(8,128)S(1)} %get-tuple-element.61.before_ref, bf16[4,160,128]{2,1,0:T(8,128)(2,1)S(1)} %pad_maximum_fusion.1.prefix_ref), custom_call_target="tpu_custom_call" | custom-call | flops 167772160 | bytes 4194304 | tf_op jit(solution)/shard_map/carry/pallas_call | solution.py:308
  38.5 0.1 collective-permute-start.7
  38.5 1.3 %mix.4.refs_1_ = f32[1024,1024]{1,0:T(8,128)S(1)} custom-call(s32[1]{0:T(128)} %bitcast.mine_ref, bf16[2048,1024]{1,0:T(8,128)(2,1)S(1)} %get-tuple-element.43.w_ref, bf16[1024,512]{1,0:T(8,128)(2,1)S(1)} %carry.3.refs_0_, f32[1024,1024]{1,0:T(8,128)S(1)} %mix.3.refs_1_), custom_call_target="tpu_custom_call" | custom-call | flops 1073741824 | bytes 4194304 | tf_op jit(solution)/shard_map/mix/pallas_call | solution.py:325
  39.8 1.4 %collective-permute-done.7.refs_0_ = bf16[1024,512]{1,0:T(8,128)(2,1)S(1)} collective-permute-done((bf16[1024,512]{1,0:T(8,128)(2,1)S(1)}, bf16[1024,512]{1,0:T(8,128)(2,1)S(1)}, u32[]{:S(2)}, u32[]{:S(2)}) %collective-permute-start.7) | collective-permute-done | bytes 1048608 | tf_op jit(solution)/shard_map/ppermute | solution.py:338
  41.2 2.4 %mix.5 = bf16[1024,1024]{1,0:T(8,128)(2,1)} custom-call(s32[1]{0:T(128)} %bitcast.mine_ref, bf16[2048,1024]{1,0:T(8,128)(2,1)S(1)} %get-tuple-element.43.w_ref, bf16[1024,512]{1,0:T(8,128)(2,1)S(1)} %collective-permute-done.7.refs_0_, f32[1024,1024]{1,0:T(8,128)S(1)} %mix.4.refs_1_), custom_call_target="tpu_custom_call" | custom-call | flops 1073741824 | bytes 4194304 | tf_op jit(solution)/shard_map/mix/pallas_call | solution.py:325
  (13 shorter events, 0.3 us)
Async XLA Ops:
  6.9 6.5 %collective-permute-start = (bf16[2,160,128]{2,1,0:T(8,128)(2,1)S(1)}, bf16[2,160,128]{2,1,0:T(8,128)(2,1)S(1)}, u32[]{:S(2)}, u32[]{:S(2)}) collective-permute-start(bf16[2,160,128]{2,1,0:T(8,128)(2,1)S(1)} %broadcast_select_fusion.5), channel_id=1, source_target_pairs={{0,2},{2,0},{4,6},{6,4},{1,3},{3,1},{5,7},{7,5},{8,10},{10,8},{12,... | collective-permute-start | bytes 245768 | tf_op jit(solution)/shard_map/ppermute | solution.py:338
  13.4 6.5 %collective-permute-start.1 = (bf16[2,160,128]{2,1,0:T(8,128)(2,1)S(1)}, bf16[2,160,128]{2,1,0:T(8,128)(2,1)S(1)}, u32[]{:S(2)}, u32[]{:S(2)}) collective-permute-start(bf16[2,160,128]{2,1,0:T(8,128)(2,1)S(1)} %fusion), channel_id=1, source_target_pairs={{0,4},{2,6},{4,0},{6,2},{1,5},{3,7},{5,1},{7,3},{8,12},{10,14},{12... | collective-permute-start | bytes 245768 | tf_op jit(solution)/shard_map/ppermute | solution.py:338
  16.1 4.7 %collective-permute-start.3 = (bf16[2,160,128]{2,1,0:T(8,128)(2,1)S(1)}, bf16[2,160,128]{2,1,0:T(8,128)(2,1)S(1)}, u32[]{:S(2)}, u32[]{:S(2)}) collective-permute-start(bf16[2,160,128]{2,1,0:T(8,128)(2,1)S(1)} %broadcast_select_fusion.4), channel_id=1, source_target_pairs={{0,2},{2,0},{4,6},{6,4},{1,3},{3,1},{5,7},{7,5},{8,10},{10,8},{12,... | collective-permute-start | bytes 245768 | tf_op jit(solution)/shard_map/ppermute | solution.py:338
  19.9 4.5 %collective-permute-start.2 = (bf16[2,160,128]{2,1,0:T(8,128)(2,1)S(1)}, bf16[2,160,128]{2,1,0:T(8,128)(2,1)S(1)}, u32[]{:S(2)}, u32[]{:S(2)}) collective-permute-start(bf16[2,160,128]{2,1,0:T(8,128)(2,1)S(1)} %fusion.1), channel_id=1, source_target_pairs={{0,2},{2,0},{4,6},{6,4},{1,3},{3,1},{5,7},{7,5},{8,10},{10,8},{12,... | collective-permute-start | bytes 245768 | tf_op jit(solution)/shard_map/ppermute | solution.py:338
  25.4 7.6 %collective-permute-start.5 = (bf16[1024,512]{1,0:T(8,128)(2,1)S(1)}, bf16[1024,512]{1,0:T(8,128)(2,1)S(1)}, u32[]{:S(2)}, u32[]{:S(2)}) collective-permute-start(bf16[1024,512]{1,0:T(8,128)(2,1)S(1)} %carry.2.refs_0_), channel_id=1, source_target_pairs={{0,1},{1,0},{2,3},{3,2},{4,5},{5,4},{6,7},{7,6},{8,9},{9,8},{10,11... | collective-permute-start | bytes 3145736 | tf_op jit(solution)/shard_map/ppermute | solution.py:338
  25.4 7.5 %collective-permute-start.4 = (bf16[2,160,128]{2,1,0:T(8,128)(2,1)S(1)}, bf16[2,160,128]{2,1,0:T(8,128)(2,1)S(1)}, u32[]{:S(2)}, u32[]{:S(2)}) collective-permute-start(bf16[2,160,128]{2,1,0:T(8,128)(2,1)S(1)} %fusion.4), channel_id=1, source_target_pairs={{0,4},{2,6},{4,0},{6,2},{1,5},{3,7},{5,1},{7,3},{8,12},{10,14},{12... | collective-permute-start | bytes 245768 | tf_op jit(solution)/shard_map/ppermute | solution.py:338
  33.0 4.5 %collective-permute-start.6 = (bf16[2,160,128]{2,1,0:T(8,128)(2,1)S(1)}, bf16[2,160,128]{2,1,0:T(8,128)(2,1)S(1)}, u32[]{:S(2)}, u32[]{:S(2)}) collective-permute-start(bf16[2,160,128]{2,1,0:T(8,128)(2,1)S(1)} %fusion.5), channel_id=1, source_target_pairs={{0,2},{2,0},{4,6},{6,4},{1,3},{3,1},{5,7},{7,5},{8,10},{10,8},{12,... | collective-permute-start | bytes 245768 | tf_op jit(solution)/shard_map/ppermute | solution.py:338
  38.5 2.7 %collective-permute-start.7 = (bf16[1024,512]{1,0:T(8,128)(2,1)S(1)}, bf16[1024,512]{1,0:T(8,128)(2,1)S(1)}, u32[]{:S(2)}, u32[]{:S(2)}) collective-permute-start(bf16[1024,512]{1,0:T(8,128)(2,1)S(1)} %carry.3.refs_0_), channel_id=1, source_target_pairs={{0,1},{1,0},{2,3},{3,2},{4,5},{5,4},{6,7},{7,6},{8,9},{9,8},{10,11... | collective-permute-start | bytes 3145736 | tf_op jit(solution)/shard_map/ppermute | solution.py:338
